TPU v7x, 32 devices: a whole 2x2x4 slice. The times are simulated.
32 devices in a mesh: section: 2 (over core), ctx: 4 (over y, x), wt: 4 (over z).
Axes of the slice: x: 2, y: 2, z: 4, core: 2. Of those that a mesh axis runs over, the one named last changes fastest.
Arguments:
- inputs: bfloat16 [2, 1024, 576], P(None, ('ctx', 'wt')), may hold values from -6 to 6
- doc_start: int32 [2, 1024], replicated, may hold values from 0 to 1791, as said below
- attn_gain: float32 [2, 576], P('section'), may hold values from 0.25 to 1.75
- w_q: bfloat16 [2, 576, 576], P('section', 'wt'), may hold values from -0.25 to 0.25
- key_projection: bfloat16 [2, 576, 192], P('section', 'wt'), may hold values from -0.25 to 0.25
- value_projection: bfloat16 [2, 576, 192], P('section', 'wt'), may hold values from -0.25 to 0.25
- w_o: bfloat16 [2, 576, 576], P('section', 'wt'), may hold values from -1.5 to 1.5
- mlp_gain: float32 [2, 576], P('section'), may hold values from 0.25 to 1.75
- w_gate: bfloat16 [2, 576, 1536], P('section', None, 'wt'), may hold values from -0.25 to 0.25
- w_up: bfloat16 [2, 576, 1536], P('section', None, 'wt'), may hold values from -0.25 to 0.25
- w_down: bfloat16 [2, 1536, 576], P('section', 'wt'), may hold values from -0.15625 to 0.15625
- cotangent: float32 [2, 1024, 576], P(None, ('ctx', 'wt')), may hold values from -6 to 6
Outputs:
- acts: bfloat16 [2, 2, 1024, 576], P('section', None, ('ctx', 'wt'))
- dacts: bfloat16 [2, 2, 1024, 576], P('section', None, ('ctx', 'wt'))
- grad_attn_gain: float32 [2, 576], P('section', 'wt')
- grad_w_q: float32 [2, 576, 576], P('section', 'wt')
- grad_w_k: float32 [2, 576, 192], P('section', 'wt')
- grad_w_v: float32 [2, 576, 192], P('section', 'wt')
- grad_w_o: float32 [2, 576, 576], P('section', 'wt')
- grad_mlp_gain: float32 [2, 576], P('section', 'wt')
- grad_w_gate: float32 [2, 576, 1536], P('section', None, 'wt')
- grad_w_up: float32 [2, 576, 1536], P('section', None, 'wt')
- grad_w_down: float32 [2, 1536, 576], P('section', 'wt')
Inputs may be any that keep to these rules, and one draw needn't show every extreme that they name: `doc_start`: doc_start_i is the first position of token i's document in the sequence of 2048 tokens: never above i, never falling along the sequence, equal within a document; three documents, the last beginning at position 1791.
All inputs are finite; a program needn't handle non-finite values.
Results may differ from a plain program's by a relative error of at most 0.028.
Values may be sent and summed in bfloat16 or wider, within the bound.
A program may use at most 128 MiB of HBM per device.

v0:
```python
import math

import jax
import jax.numpy as jnp
from jax import lax
from jax.sharding import PartitionSpec as P

QUERY_HEAD_COUNT = 9
KEY_VALUE_HEADS = 3
HEAD_DIMENSION = 64


EPSILON = 1e-05
THETA = 100000.0
MASKED_FLOOR = -1e30


def from_behind(x, axis, by):
    peers = lax.axis_size(axis)
    return lax.ppermute(x, axis, [(i, (i + by) % peers) for i in range(peers)])


def rope_tables(rotary):
    half_size = HEAD_DIMENSION // 2
    inverse = 1.0 / THETA ** (jnp.arange(half_size).astype(jnp.float32) * 2.0 / HEAD_DIMENSION)
    angles = rotary[:, None] * inverse[None, :]
    return (
        jnp.concatenate([jnp.cos(angles), jnp.cos(angles)], -1),
        jnp.concatenate([jnp.sin(angles), jnp.sin(angles)], -1),
    )


def apply_rotation(value_matrix, cosine_values, sine_values):
    half_size = value_matrix.shape[-1] // 2
    turned = jnp.concatenate([-value_matrix[..., half_size:], value_matrix[..., :half_size]], -1)
    return value_matrix * cosine_values[:, None, :] + turned * sine_values[:, None, :]


def reverse_rotation(grads, cosine_values, sine_values):
    half_size = grads.shape[-1] // 2
    scaled = grads * sine_values[:, None, :]
    turned = jnp.concatenate([scaled[..., half_size:], -scaled[..., :half_size]], -1)
    return grads * cosine_values[:, None, :] + turned


def row_product(left_matrix, right_matrix):
    return lax.dot_general(
        left_matrix, right_matrix, (((0,), (0,)), ((), ())), preferred_element_type=jnp.float32
    )


def back_product(left_matrix, right_matrix):
    return lax.dot_general(
        left_matrix, right_matrix, (((1,), (1,)), ((), ())), preferred_element_type=jnp.float32
    )


def masked_scores(heads_of_queries, heads_of_keys, query_pos, query_doc, key_pos):
    scores = (
        jnp.einsum(
            "qhge,khe->hgqk", heads_of_queries, heads_of_keys, preferred_element_type=jnp.float32
        )
        * 0.125
    )
    allowed = (key_pos[None, :] <= query_pos[:, None]) & (key_pos[None, :] >= query_doc[:, None])
    return jnp.where(allowed[None, None], scores, MASKED_FLOOR)


def block_grads(
    heads_of_queries,
    query_pos,
    query_doc,
    log_total,
    head_gradients,
    delta_per_row,
    heads_of_keys,
    heads_of_values,
    key_pos,
):
    scores = masked_scores(heads_of_queries, heads_of_keys, query_pos, query_doc, key_pos)
    probabilities = jnp.exp(scores - log_total[..., None])
    grad_probs = jnp.einsum(
        "qhge,khe->hgqk", head_gradients, heads_of_values, preferred_element_type=jnp.float32
    )
    grad_scores = (probabilities * (grad_probs - delta_per_row[..., None])).astype(jnp.bfloat16)
    return (grad_scores, probabilities.astype(jnp.bfloat16))


def keep_slot(store, micro_slot, is_live, value):
    current = lax.dynamic_index_in_dim(store, micro_slot, 0, keepdims=False)
    return lax.dynamic_update_index_in_dim(store, jnp.where(is_live, value, current), micro_slot, 0)


def pass_section(value_matrix):
    return from_behind(value_matrix, "section", 1)


def local(
    inputs,
    doc_start,
    attn_gain,
    w_q,
    key_projection,
    value_projection,
    w_o,
    mlp_gain,
    w_gate,
    w_up,
    w_down,
    cotangent,
):
    micro_count, rows_of_tokens, model_width = inputs.shape
    query_groups = QUERY_HEAD_COUNT // KEY_VALUE_HEADS
    key_value_width = KEY_VALUE_HEADS * HEAD_DIMENSION
    cycle_size = lax.axis_size(("ctx", "wt"))
    place = lax.axis_index(("ctx", "wt"))
    section_index = lax.axis_index("section")
    batch_tokens = cycle_size * rows_of_tokens
    local_keys = micro_count * rows_of_tokens
    whole_keys = cycle_size * local_keys
    block_of_keys = math.gcd(whole_keys, 512)
    gain_attn = attn_gain[0]
    gain_mlp = mlp_gain[0]
    query_weight, key_weight, value_weight, out_weight = (
        lax.all_gather(w_q[0], "wt", axis=0, tiled=True),
        lax.all_gather(key_projection[0], "wt", axis=0, tiled=True),
        lax.all_gather(value_projection[0], "wt", axis=0, tiled=True),
        lax.all_gather(w_o[0], "wt", axis=0, tiled=True),
    )
    gate_weight, up_weight, down_weight = (w_gate[0], w_up[0], w_down[0])
    key_rows = jnp.arange(whole_keys, dtype=jnp.int32)
    key_rest = key_rows % local_keys
    key_pos = (
        key_rest // rows_of_tokens * batch_tokens
        + key_rows // local_keys * rows_of_tokens
        + key_rest % rows_of_tokens
    )
    row_index = jnp.arange(rows_of_tokens, dtype=jnp.int32)

    def token_setup(micro_slot):
        query_pos = micro_slot * batch_tokens + place * rows_of_tokens + row_index
        query_doc = lax.dynamic_slice(
            doc_start, (micro_slot, place * rows_of_tokens), (1, rows_of_tokens)
        )[0]
        cosine_values, sine_values = rope_tables((query_pos - query_doc).astype(jnp.float32))
        return (query_pos, query_doc, cosine_values, sine_values)

    received = jnp.zeros((rows_of_tokens, model_width), jnp.bfloat16)
    kv_cache = jnp.zeros((micro_count, rows_of_tokens, 2 * key_value_width), jnp.bfloat16)
    outputs = jnp.zeros((micro_count, rows_of_tokens, model_width), jnp.bfloat16)
    stores = ()
    for tick in range(micro_count + 1):
        micro_index = tick - section_index
        is_live = (micro_index >= 0) & (micro_index < micro_count)
        micro_slot = jnp.clip(micro_index, 0, micro_count - 1)
        section_in = jnp.where(section_index == 0, inputs[min(tick, micro_count - 1)], received)
        layer_kv_cache = kv_cache
        layer_query_pos, layer_query_doc, layer_cosine_values, layer_sine_values = token_setup(
            micro_slot
        )
        hidden = section_in.astype(jnp.float32)
        layer_inverse1 = lax.rsqrt(jnp.mean(hidden * hidden, -1, keepdims=True) + EPSILON)
        layer_normed1 = hidden * layer_inverse1
        layer_attention_input = (layer_normed1 * gain_attn).astype(jnp.bfloat16)
        layer_query_matrix = apply_rotation(
            jnp.dot(
                layer_attention_input, query_weight, preferred_element_type=jnp.float32
            ).reshape(rows_of_tokens, QUERY_HEAD_COUNT, HEAD_DIMENSION),
            layer_cosine_values,
            layer_sine_values,
        ).astype(jnp.bfloat16)
        key_matrix = apply_rotation(
            jnp.dot(layer_attention_input, key_weight, preferred_element_type=jnp.float32).reshape(
                rows_of_tokens, KEY_VALUE_HEADS, HEAD_DIMENSION
            ),
            layer_cosine_values,
            layer_sine_values,
        ).astype(jnp.bfloat16)
        value_matrix = jnp.dot(
            layer_attention_input, value_weight, preferred_element_type=jnp.float32
        ).astype(jnp.bfloat16)
        fresh_rows = jnp.concatenate(
            [key_matrix.reshape(rows_of_tokens, key_value_width), value_matrix], -1
        )
        layer_kv_cache = keep_slot(layer_kv_cache, micro_slot, is_live, fresh_rows)
        layer_key_values = lax.all_gather(
            layer_kv_cache.reshape(local_keys, 2 * key_value_width),
            ("ctx", "wt"),
            axis=0,
            tiled=True,
        )
        attend_heads_of_queries = layer_query_matrix.reshape(
            rows_of_tokens, KEY_VALUE_HEADS, query_groups, HEAD_DIMENSION
        )
        attend_query_pos = layer_query_pos
        attend_query_doc = layer_query_doc
        attend_key_values = layer_key_values

        def fold_block(carry, block_index):
            row_top, summed, accumulated = carry
            key_segment = lax.dynamic_slice_in_dim(
                attend_key_values, block_index * block_of_keys, block_of_keys, 0
            )
            slab_pos = lax.dynamic_slice_in_dim(
                key_pos, block_index * block_of_keys, block_of_keys, 0
            )
            heads_of_keys = key_segment[:, :key_value_width].reshape(
                block_of_keys, KEY_VALUE_HEADS, HEAD_DIMENSION
            )
            heads_of_values = key_segment[:, key_value_width:].reshape(
                block_of_keys, KEY_VALUE_HEADS, HEAD_DIMENSION
            )
            scores = masked_scores(
                attend_heads_of_queries, heads_of_keys, attend_query_pos, attend_query_doc, slab_pos
            )
            new_top = jnp.maximum(row_top, jnp.max(scores, -1))
            factor = jnp.exp(row_top - new_top)
            weights = jnp.exp(scores - new_top[..., None])
            summed = summed * factor + jnp.sum(weights, -1)
            accumulated = accumulated * factor[..., None] + jnp.einsum(
                "hgqk,khe->hgqe",
                weights.astype(jnp.bfloat16),
                heads_of_values,
                preferred_element_type=jnp.float32,
            )
            return ((new_top, summed, accumulated), None)

        start_state = (
            jnp.full((KEY_VALUE_HEADS, query_groups, rows_of_tokens), MASKED_FLOOR, jnp.float32),
            jnp.zeros((KEY_VALUE_HEADS, query_groups, rows_of_tokens), jnp.float32),
            jnp.zeros((KEY_VALUE_HEADS, query_groups, rows_of_tokens, HEAD_DIMENSION), jnp.float32),
        )
        final_state, unused = lax.scan(
            fold_block, start_state, jnp.arange(whole_keys // block_of_keys)
        )
        row_top, summed, accumulated = final_state
        attend_blended_output = (
            (accumulated / summed[..., None])
            .transpose(2, 0, 1, 3)
            .reshape(rows_of_tokens, QUERY_HEAD_COUNT * HEAD_DIMENSION)
            .astype(jnp.bfloat16)
        )
        layer_log_total = row_top + jnp.log(summed)
        residual = hidden + jnp.dot(
            attend_blended_output, out_weight, preferred_element_type=jnp.float32
        )
        layer_inverse2 = lax.rsqrt(jnp.mean(residual * residual, -1, keepdims=True) + EPSILON)
        layer_normed2 = residual * layer_inverse2
        mlp_in = (layer_normed2 * gain_mlp).astype(jnp.bfloat16)
        layer_mlp_rows = lax.all_gather(mlp_in, "wt", axis=0, tiled=True)
        layer_gate_pre = jnp.dot(layer_mlp_rows, gate_weight, preferred_element_type=jnp.float32)
        layer_up_pre = jnp.dot(layer_mlp_rows, up_weight, preferred_element_type=jnp.float32)
        layer_activated = (layer_gate_pre * jax.nn.sigmoid(layer_gate_pre) * layer_up_pre).astype(
            jnp.bfloat16
        )
        branch_out = jnp.dot(layer_activated, down_weight, preferred_element_type=jnp.float32)
        mlp_out = lax.psum_scatter(
            branch_out.astype(jnp.bfloat16), "wt", scatter_dimension=0, tiled=True
        ).astype(jnp.float32)
        result = (residual + mlp_out).astype(jnp.bfloat16)
        saved_state = (
            layer_normed1,
            layer_inverse1,
            layer_attention_input,
            layer_query_matrix,
            attend_blended_output,
            layer_log_total,
            layer_key_values,
            layer_normed2,
            layer_inverse2,
            layer_mlp_rows,
            layer_gate_pre,
            layer_up_pre,
            layer_activated,
        )
        result, saved_state, kv_cache = (result, saved_state, layer_kv_cache)
        if tick == 0:
            stores = tuple(
                (jnp.zeros((micro_count,) + item.shape, item.dtype) for item in saved_state)
            )
        stores = tuple(
            (
                keep_slot(store, micro_slot, is_live, item)
                for store, item in zip(stores, saved_state)
            )
        )
        outputs = keep_slot(outputs, micro_slot, is_live, result)
        if tick < micro_count:
            received = pass_section(result)
    grad_received = jnp.zeros((rows_of_tokens, model_width), jnp.bfloat16)
    key_grad_store = jnp.zeros((micro_count, rows_of_tokens, 2 * key_value_width), jnp.float32)
    input_grads = jnp.zeros((micro_count, rows_of_tokens, model_width), jnp.bfloat16)
    grad_query_w = jnp.zeros(query_weight.shape, jnp.float32)
    grad_key_w = jnp.zeros(key_weight.shape, jnp.float32)
    grad_value_w = jnp.zeros(value_weight.shape, jnp.float32)
    grad_out_w = jnp.zeros(out_weight.shape, jnp.float32)
    grad_gate_w = jnp.zeros(gate_weight.shape, jnp.float32)
    grad_up_w = jnp.zeros(up_weight.shape, jnp.float32)
    grad_down_w = jnp.zeros(down_weight.shape, jnp.float32)
    grad_gain_attn = jnp.zeros((model_width,), jnp.float32)
    grad_gain_mlp = jnp.zeros((model_width,), jnp.float32)
    for tick in range(micro_count + 1):
        micro_index = micro_count - tick - section_index
        is_live = (micro_index >= 0) & (micro_index < micro_count)
        micro_slot = jnp.clip(micro_index, 0, micro_count - 1)
        live_weight = is_live.astype(jnp.float32)
        (
            normed1,
            inverse1,
            attention_input,
            query_matrix,
            blended_output,
            log_total,
            key_values,
            normed2,
            inverse2,
            mlp_rows,
            gate_pre,
            up_pre,
            activated,
        ) = tuple(
            (lax.dynamic_index_in_dim(store, micro_slot, 0, keepdims=False) for store in stores)
        )
        query_pos, query_doc, cosine_values, sine_values = token_setup(micro_slot)
        upstream = jnp.where(
            section_index == 1,
            lax.dynamic_index_in_dim(cotangent, micro_slot, 0, keepdims=False),
            grad_received.astype(jnp.float32),
        )
        out_grad = upstream.astype(jnp.bfloat16)
        out_rows = lax.all_gather(out_grad, "wt", axis=0, tiled=True)
        grad_down_w = grad_down_w + live_weight * row_product(activated, out_rows)
        grad_activated = back_product(out_rows, down_weight)
        sigmoid_gate = jax.nn.sigmoid(gate_pre)
        grad_gate_rows = (
            grad_activated * up_pre * sigmoid_gate * (1.0 + gate_pre * (1.0 - sigmoid_gate))
        ).astype(jnp.bfloat16)
        grad_up_rows = (grad_activated * gate_pre * sigmoid_gate).astype(jnp.bfloat16)
        grad_gate_w = grad_gate_w + live_weight * row_product(mlp_rows, grad_gate_rows)
        grad_up_w = grad_up_w + live_weight * row_product(mlp_rows, grad_up_rows)
        mlp_term = back_product(grad_gate_rows, gate_weight) + back_product(grad_up_rows, up_weight)
        grad_mlp_in = lax.psum_scatter(
            mlp_term.astype(jnp.bfloat16), "wt", scatter_dimension=0, tiled=True
        ).astype(jnp.float32)
        grad_gain_mlp = grad_gain_mlp + live_weight * jnp.sum(grad_mlp_in * normed2, 0)
        scaled2 = grad_mlp_in * gain_mlp
        grad_residual = upstream + inverse2 * (
            scaled2 - normed2 * jnp.mean(scaled2 * normed2, -1, keepdims=True)
        )
        residual_grad = grad_residual.astype(jnp.bfloat16)
        grad_out_w = grad_out_w + live_weight * row_product(blended_output, residual_grad)
        attention_gradient = back_product(residual_grad, out_weight).astype(jnp.bfloat16)
        delta_per_row = jnp.sum(
            (attention_gradient.astype(jnp.float32) * blended_output.astype(jnp.float32)).reshape(
                rows_of_tokens, KEY_VALUE_HEADS, query_groups, HEAD_DIMENSION
            ),
            -1,
        ).transpose(1, 2, 0)
        heads_of_queries = query_matrix.reshape(
            rows_of_tokens, KEY_VALUE_HEADS, query_groups, HEAD_DIMENSION
        )
        head_gradients = attention_gradient.reshape(
            rows_of_tokens, KEY_VALUE_HEADS, query_groups, HEAD_DIMENSION
        )

        def grad_block(carry, block_index):
            key_segment = lax.dynamic_slice_in_dim(
                key_values, block_index * block_of_keys, block_of_keys, 0
            )
            slab_pos = lax.dynamic_slice_in_dim(
                key_pos, block_index * block_of_keys, block_of_keys, 0
            )
            heads_of_keys = key_segment[:, :key_value_width].reshape(
                block_of_keys, KEY_VALUE_HEADS, HEAD_DIMENSION
            )
            heads_of_values = key_segment[:, key_value_width:].reshape(
                block_of_keys, KEY_VALUE_HEADS, HEAD_DIMENSION
            )
            grad_scores, probabilities = block_grads(
                heads_of_queries,
                query_pos,
                query_doc,
                log_total,
                head_gradients,
                delta_per_row,
                heads_of_keys,
                heads_of_values,
                slab_pos,
            )
            carry = (
                carry
                + jnp.einsum(
                    "hgqk,khe->qhge", grad_scores, heads_of_keys, preferred_element_type=jnp.float32
                )
                * 0.125
            )
            grad_key_heads = (
                jnp.einsum(
                    "hgqk,qhge->khe",
                    grad_scores,
                    heads_of_queries,
                    preferred_element_type=jnp.float32,
                )
                * 0.125
            )
            grad_value_heads = jnp.einsum(
                "hgqk,qhge->khe", probabilities, head_gradients, preferred_element_type=jnp.float32
            )
            return (
                carry,
                jnp.concatenate(
                    [
                        grad_key_heads.reshape(block_of_keys, key_value_width),
                        grad_value_heads.reshape(block_of_keys, key_value_width),
                    ],
                    -1,
                ),
            )

        grad_query, key_terms = lax.scan(
            grad_block,
            jnp.zeros((rows_of_tokens, KEY_VALUE_HEADS, query_groups, HEAD_DIMENSION), jnp.float32),
            jnp.arange(whole_keys // block_of_keys),
        )
        grad_query, key_terms = (grad_query, key_terms.reshape(whole_keys, 2 * key_value_width))
        own_grads = lax.psum_scatter(key_terms, ("ctx", "wt"), scatter_dimension=0, tiled=True)
        key_grad_store = key_grad_store + live_weight * own_grads.reshape(
            micro_count, rows_of_tokens, 2 * key_value_width
        )
        local_rows_owned = lax.dynamic_index_in_dim(key_grad_store, micro_slot, 0, keepdims=False)
        key_gradients = (
            reverse_rotation(
                local_rows_owned[:, :key_value_width].reshape(
                    rows_of_tokens, KEY_VALUE_HEADS, HEAD_DIMENSION
                ),
                cosine_values,
                sine_values,
            )
            .astype(jnp.bfloat16)
            .reshape(rows_of_tokens, key_value_width)
        )
        value_gradients = local_rows_owned[:, key_value_width:].astype(jnp.bfloat16)
        grad_queries = (
            reverse_rotation(
                grad_query.reshape(rows_of_tokens, QUERY_HEAD_COUNT, HEAD_DIMENSION),
                cosine_values,
                sine_values,
            )
            .astype(jnp.bfloat16)
            .reshape(rows_of_tokens, QUERY_HEAD_COUNT * HEAD_DIMENSION)
        )
        grad_query_w = grad_query_w + live_weight * row_product(attention_input, grad_queries)
        grad_key_w = grad_key_w + live_weight * row_product(attention_input, key_gradients)
        grad_value_w = grad_value_w + live_weight * row_product(attention_input, value_gradients)
        grad_attn_in = (
            back_product(grad_queries, query_weight)
            + back_product(key_gradients, key_weight)
            + back_product(value_gradients, value_weight)
        )
        grad_gain_attn = grad_gain_attn + live_weight * jnp.sum(grad_attn_in * normed1, 0)
        scaled1 = grad_attn_in * gain_attn
        input_grad = (
            grad_residual
            + inverse1 * (scaled1 - normed1 * jnp.mean(scaled1 * normed1, -1, keepdims=True))
        ).astype(jnp.bfloat16)
        input_grads = keep_slot(input_grads, micro_slot, is_live, input_grad)
        if tick < micro_count:
            grad_received = pass_section(input_grad)
    share_query, share_key, share_value, share_out, share_gain_attn, share_gain_mlp = (
        lax.psum_scatter(
            grad_query_w.astype(jnp.bfloat16), "wt", scatter_dimension=0, tiled=True
        ).astype(jnp.float32),
        lax.psum_scatter(
            grad_key_w.astype(jnp.bfloat16), "wt", scatter_dimension=0, tiled=True
        ).astype(jnp.float32),
        lax.psum_scatter(
            grad_value_w.astype(jnp.bfloat16), "wt", scatter_dimension=0, tiled=True
        ).astype(jnp.float32),
        lax.psum_scatter(
            grad_out_w.astype(jnp.bfloat16), "wt", scatter_dimension=0, tiled=True
        ).astype(jnp.float32),
        lax.psum_scatter(
            grad_gain_attn.astype(jnp.bfloat16), "wt", scatter_dimension=0, tiled=True
        ).astype(jnp.float32),
        lax.psum_scatter(
            grad_gain_mlp.astype(jnp.bfloat16), "wt", scatter_dimension=0, tiled=True
        ).astype(jnp.float32),
    )
    share_gate, share_lift, share_down = (grad_gate_w, grad_up_w, grad_down_w)
    (
        total_query,
        total_key,
        total_value,
        total_out,
        total_gain_attn,
        total_gain_mlp,
        total_gate,
        total_lift,
        total_down,
    ) = (
        lax.psum(share_query.astype(jnp.bfloat16), "ctx").astype(jnp.float32),
        lax.psum(share_key.astype(jnp.bfloat16), "ctx").astype(jnp.float32),
        lax.psum(share_value.astype(jnp.bfloat16), "ctx").astype(jnp.float32),
        lax.psum(share_out.astype(jnp.bfloat16), "ctx").astype(jnp.float32),
        lax.psum(share_gain_attn.astype(jnp.bfloat16), "ctx").astype(jnp.float32),
        lax.psum(share_gain_mlp.astype(jnp.bfloat16), "ctx").astype(jnp.float32),
        lax.psum(share_gate.astype(jnp.bfloat16), "ctx").astype(jnp.float32),
        lax.psum(share_lift.astype(jnp.bfloat16), "ctx").astype(jnp.float32),
        lax.psum(share_down.astype(jnp.bfloat16), "ctx").astype(jnp.float32),
    )
    return (
        outputs[None],
        input_grads[None],
        total_gain_attn[None],
        total_query[None],
        total_key[None],
        total_value[None],
        total_out[None],
        total_gain_mlp[None],
        total_gate[None],
        total_lift[None],
        total_down[None],
    )


def solution(mesh):
    in_specs = (
        P(None, ("ctx", "wt"), None),
        P(),
        P("section", None),
        P("section", "wt", None),
        P("section", "wt", None),
        P("section", "wt", None),
        P("section", "wt", None),
        P("section", None),
        P("section", None, "wt"),
        P("section", None, "wt"),
        P("section", "wt", None),
        P(None, ("ctx", "wt"), None),
    )
    out_specs = (
        P("section", None, ("ctx", "wt"), None),
        P("section", None, ("ctx", "wt"), None),
        P("section", "wt"),
        P("section", "wt", None),
        P("section", "wt", None),
        P("section", "wt", None),
        P("section", "wt", None),
        P("section", "wt"),
        P("section", None, "wt"),
        P("section", None, "wt"),
        P("section", "wt", None),
    )
    return jax.shard_map(local, mesh=mesh, in_specs=in_specs, out_specs=out_specs, check_vma=False)
```

profile of v0, /device:TPU:0, one launch (start us, length us, event | category | flops | bytes accessed | tf_op | source)
XLA Modules:
  0.0 1287.4 jit_solution(3895218666047068974)
XLA Ops:
  10.6 15.9 %all-gather = bf16[1,576,192]{2,1,0:T(8,128)(2,1)S(1)} all-gather(bf16[1,144,192]{2,1,0:T(8,128)(2,1)} %param.28), channel_id=2, replica_groups=mesh['section'=2,'ctx'=4,'wt'=4] {'wt'}, dimensions={1}, use_global_device_ids=true | all-gather | bytes 276480 | tf_op jit(solution)/shard_map/all_gather | solution.py:126
  27.2 14.9 %all-gather.1 = bf16[1,576,192]{2,1,0:T(8,128)(2,1)S(1)} all-gather(bf16[1,144,192]{2,1,0:T(8,128)(2,1)S(1)} %copy-done.231), channel_id=3, replica_groups=mesh['section'=2,'ctx'=4,'wt'=4] {'wt'}, dimensions={1}, use_global_device_ids=true | all-gather | bytes 276480 | tf_op jit(solution)/shard_map/all_gather | solution.py:127
  43.3 17.4 %all-gather.2 = bf16[1,576,576]{2,1,0:T(8,128)(2,1)S(1)} all-gather(bf16[1,144,576]{2,1,0:T(8,128)(2,1)S(1)} %copy-done.223), channel_id=4, replica_groups=mesh['section'=2,'ctx'=4,'wt'=4] {'wt'}, dimensions={1}, use_global_device_ids=true | all-gather | bytes 829440 | tf_op jit(solution)/shard_map/all_gather | solution.py:125
  63.2 18.7 %all-gather.3 = bf16[1,576,576]{2,1,0:T(8,128)(2,1)S(1)} all-gather(bf16[1,144,576]{2,1,0:T(8,128)(2,1)S(1)} %copy-done.224), channel_id=5, replica_groups=mesh['section'=2,'ctx'=4,'wt'=4] {'wt'}, dimensions={1}, use_global_device_ids=true | all-gather | bytes 829440 | tf_op jit(solution)/shard_map/all_gather | solution.py:128
  81.9 22.3 %all-gather.8.cloned.1.call-done = bf16[2048,384]{0,1:T(8,128)(2,1)} async-done(((bf16[128,384]{0,1:T(8,128)(2,1)}), bf16[2048,384]{0,1:T(8,128)(2,1)}) %all-gather.8.cloned.1.call-update) | async-done | bytes 1572880 | tf_op jit(solution)/shard_map/all_gather | solution.py:186
  104.1 22.4 %while.84 = (s32[]{:T(128)}, f32[3,3,64]{2,1,0:T(4,128)S(1)}, f32[3,3,64]{2,1,0:T(4,128)S(1)}, f32[3,3,64,64]{3,2,1,0:T(8,128)}, s32[4]{0:T(128)S(1)}, /*index=5...) while((s32[]{:T(128)}, f32[3,3,64]{2,1,0:T(4,128)S(1)}, ...), condition=%wide.region_4.5_spmd.clone, body=%wide.region_1.4_spmd.clone.sunk | while | flops 77773704 | bytes 6376487 | solution.py:233
  129.4 14.7 %all_gather.44 = bf16[256,576]{1,0:T(8,128)(2,1)S(1)} all-gather(bf16[64,576]{1,0:T(8,128)(2,1)S(1)} %multiply_convert_fusion.5), channel_id=1, replica_groups=mesh['section'=2,'ctx'=4,'wt'=4] {'wt'}, dimensions={0}, use_global_device_ids=true | all-gather | bytes 368640 | tf_op jit(solution)/shard_map/all_gather | solution.py:250
  149.6 16.6 %all_gather.49 = bf16[256,576]{1,0:T(8,128)(2,1)} all-gather(bf16[64,576]{1,0:T(8,128)(2,1)S(1)} %bitcast_convert_fusion), channel_id=1, replica_groups=mesh['section'=2,'ctx'=4,'wt'=4] {'wt'}, dimensions={0}, use_global_device_ids=true | all-gather | bytes 368640 | tf_op jit(solution)/shard_map/all_gather | solution.py:331
  170.3 1.8 copy.297
  179.5 1.8 constant_dynamic-slice_fusion.39
  183.0 1.8 constant_dynamic-slice_fusion.41
  192.0 41.4 %all-gather.10.cloned.1.call-done = bf16[2048,384]{0,1:T(8,128)(2,1)} async-done(((bf16[128,384]{0,1:T(8,128)(2,1)}), bf16[2048,384]{0,1:T(8,128)(2,1)}) %all-gather.10.cloned.1.call-update) | async-done | bytes 1572880 | tf_op jit(solution)/shard_map/all_gather | solution.py:186
  233.9 33.1 %while.85 = (s32[]{:T(128)}, f32[3,3,64]{2,1,0:T(4,128)}, f32[3,3,64]{2,1,0:T(4,128)}, f32[3,3,64,64]{3,2,1,0:T(8,128)}, s32[4]{0:T(128)}, /*index=5*/s32[2048]{...) while((s32[]{:T(128)}, f32[3,3,64]{2,1,0:T(4,128)}, ...), condition=%wide.region_11.12_spmd.clone, body=%wide.region_8.11_spmd.clone.sunk | while | flops 77773704 | bytes 6404219 | solution.py:233
  269.1 14.8 %all_gather.46 = bf16[256,576]{1,0:T(8,128)(2,1)S(1)} all-gather(bf16[64,576]{1,0:T(8,128)(2,1)S(1)} %multiply_convert_fusion.4), channel_id=1, replica_groups=mesh['section'=2,'ctx'=4,'wt'=4] {'wt'}, dimensions={0}, use_global_device_ids=true | all-gather | bytes 368640 | tf_op jit(solution)/shard_map/all_gather | solution.py:250
  287.6 2.0 fusion.282
  290.6 15.7 %reduce-scatter.16.cloned.1.call-done = bf16[64,576]{1,0:T(8,128)(2,1)} async-done(((bf16[256,576]{1,0:T(8,128)(2,1)}), bf16[64,576]{1,0:T(8,128)(2,1)}) %reduce-scatter.16.cloned.1.call-update) | async-done | bytes 73744 | tf_op jit(solution)/shard_map/reduce_scatter | solution.py:257
  306.3 1.6 fusion.325
  307.9 1.7 constant_dynamic-slice_fusion.6
  315.4 1.8 constant_dynamic-slice_fusion.40
  317.2 1.8 constant_dynamic-slice_fusion.38
  319.2 3.3 bitcast_dynamic-update-slice_fusion.1
  322.5 2.8 constant_dynamic-slice_fusion.31
  327.7 42.3 %all-gather.12.cloned.1.call-done = bf16[2048,384]{0,1:T(8,128)(2,1)} async-done(((bf16[128,384]{0,1:T(8,128)(2,1)}), bf16[2048,384]{0,1:T(8,128)(2,1)}) %all-gather.12.cloned.1.call-update) | async-done | bytes 1572880 | tf_op jit(solution)/shard_map/all_gather | solution.py:186
  370.4 30.1 %while.86 = (s32[]{:T(128)}, f32[3,3,64]{2,1,0:T(4,128)}, f32[3,3,64]{2,1,0:T(4,128)}, f32[3,3,64,64]{3,2,1,0:T(8,128)S(1)}, s32[4]{0:T(128)}, /*index=5*/s32[20...) while((s32[]{:T(128)}, f32[3,3,64]{2,1,0:T(4,128)}, ...), condition=%wide.region_18.19_spmd.clone, body=%wide.region_15.18_spmd.clone.sunk | while | flops 77773704 | bytes 5224515 | solution.py:233
  401.6 1.6 select_dynamic-update-slice_fusion
  403.2 1.9 constant_dynamic-slice_fusion.13
  406.0 14.8 %all_gather.48 = bf16[256,576]{1,0:T(8,128)(2,1)S(1)} all-gather(bf16[64,576]{1,0:T(8,128)(2,1)S(1)} %multiply_convert_fusion.3), channel_id=1, replica_groups=mesh['section'=2,'ctx'=4,'wt'=4] {'wt'}, dimensions={0}, use_global_device_ids=true | all-gather | bytes 368640 | tf_op jit(solution)/shard_map/all_gather | solution.py:250
  428.1 3.3 bitcast_dynamic-update-slice_fusion
  432.9 4.8 dynamic-slice_bitcast_fusion
  437.7 8.6 reduce-scatter.20.cloned.1.call-done
  450.2 1.9 broadcast.851.clone2
  452.2 33.5 %while.87 = (s32[]{:T(128)}, f32[64,3,3,64]{0,3,2,1:T(8,128)}, f32[4,512,384]{2,1,0:T(8,128)}, s32[4]{0:T(128)S(1)}, bf16[2048,384]{0,1:T(8,128)(2,1)}, /*index=...) while((s32[]{:T(128)}, f32[64,3,3,64]{0,3,2,1:T(8,128)}, ...), condition=%wide.region_25.26_spmd.clone, body=%wide.region_24.25_spmd.clone.sunk | while | flops 191311936 | bytes 14921873 | solution.py:420
  491.1 125.4 %reduce-scatter.22.cloned.1.call-done = f32[128,384]{1,0:T(8,128)} async-done(((f32[2048,384]{1,0:T(8,128)}), f32[128,384]{1,0:T(8,128)}) %reduce-scatter.22.cloned.1.call-update) | async-done | bytes 196624 | tf_op jit(solution)/shard_map/reduce_scatter | solution.py:426
  619.3 2.0 fusion.278
  623.4 14.4 %all_gather.50 = bf16[256,576]{1,0:T(8,128)(2,1)S(1)} all-gather(bf16[64,576]{1,0:T(8,128)(2,1)S(1)} %fusion.310), channel_id=1, replica_groups=mesh['section'=2,'ctx'=4,'wt'=4] {'wt'}, dimensions={0}, use_global_device_ids=true | all-gather | bytes 368640 | tf_op jit(solution)/shard_map/all_gather | solution.py:331
  641.1 19.7 %reduce-scatter.24.cloned.1.call-done = bf16[64,576]{1,0:T(8,128)(2,1)} async-done(((bf16[256,576]{1,0:T(8,128)(2,1)}), bf16[64,576]{1,0:T(8,128)(2,1)}) %reduce-scatter.24.cloned.1.call-update) | async-done | bytes 73744 | tf_op jit(solution)/shard_map/reduce_scatter | solution.py:342
  665.3 1.9 broadcast.851.clone2.1
  667.2 38.7 %while.88 = (s32[]{:T(128)}, f32[64,3,3,64]{0,3,2,1:T(8,128)}, f32[4,512,384]{2,1,0:T(8,128)}, s32[4]{0:T(128)}, bf16[2048,384]{0,1:T(8,128)(2,1)}, /*index=5*/s...) while((s32[]{:T(128)}, f32[64,3,3,64]{0,3,2,1:T(8,128)}, ...), condition=%wide.region_32.33_spmd.clone, body=%wide.region_31.32_spmd.clone.sunk | while | flops 191311936 | bytes 13742169 | solution.py:420
  684.0 2.1 fusion.634
  693.9 2.1 fusion.634
  703.8 2.1 fusion.634
  709.5 1.7 fusion.187
  711.3 1.7 fusion.185
  713.0 123.7 %reduce-scatter.26.cloned.1.call-done = f32[128,384]{1,0:T(8,128)} async-done(((f32[2048,384]{1,0:T(8,128)}), f32[128,384]{1,0:T(8,128)}) %reduce-scatter.26.cloned.1.call-update) | async-done | bytes 196624 | tf_op jit(solution)/shard_map/reduce_scatter | solution.py:426
  842.6 14.1 %all_gather.51 = bf16[256,576]{1,0:T(8,128)(2,1)S(1)} all-gather(bf16[64,576]{1,0:T(8,128)(2,1)S(1)} %fusion.311), channel_id=1, replica_groups=mesh['section'=2,'ctx'=4,'wt'=4] {'wt'}, dimensions={0}, use_global_device_ids=true | all-gather | bytes 368640 | tf_op jit(solution)/shard_map/all_gather | solution.py:331
  860.2 19.6 %reduce-scatter.28.cloned.1.call-done = bf16[64,576]{1,0:T(8,128)(2,1)} async-done(((bf16[256,576]{1,0:T(8,128)(2,1)}), bf16[64,576]{1,0:T(8,128)(2,1)}) %reduce-scatter.28.cloned.1.call-update) | async-done | bytes 73744 | tf_op jit(solution)/shard_map/reduce_scatter | solution.py:342
  882.8 1.9 broadcast.851.clone
  884.7 30.6 %while.89 = (s32[]{:T(128)}, f32[64,3,3,64]{0,3,2,1:T(8,128)}, f32[4,512,384]{2,1,0:T(8,128)}, s32[4]{0:T(128)S(1)}, bf16[2048,384]{0,1:T(8,128)(2,1)}, /*index=...) while((s32[]{:T(128)}, f32[64,3,3,64]{0,3,2,1:T(8,128)}, ...), condition=%wide.region_39.40_spmd.clone, body=%wide.region_38.39_spmd.clone.sunk | while | flops 191311936 | bytes 12866777 | solution.py:420
  897.5 2.0 fusion.650
  905.4 2.0 fusion.650
  913.3 2.0 fusion.650
  921.4 1.7 fusion.184
  924.2 121.7 %reduce-scatter.30.cloned.1.call-done = f32[128,384]{1,0:T(8,128)} async-done(((f32[2048,384]{1,0:T(8,128)}), f32[128,384]{1,0:T(8,128)}) %reduce-scatter.30.cloned.1.call-update) | async-done | bytes 196624 | tf_op jit(solution)/shard_map/reduce_scatter | solution.py:426
  1065.1 1.7 fusion.70
  1071.0 10.6 all-reduce.2
  1082.9 8.6 reduce-scatter.34.cloned.1.call-done
  1092.7 22.2 %reduce-scatter.38.cloned.1.call-done = bf16[144,576]{1,0:T(8,128)(2,1)} async-done(((bf16[576,576]{1,0:T(8,128)(2,1)}), bf16[144,576]{1,0:T(8,128)(2,1)}) %reduce-scatter.38.cloned.1.call-update) | async-done | bytes 165904 | tf_op jit(solution)/shard_map/reduce_scatter | solution.py:479
  1115.0 25.0 %reduce-scatter.32.cloned.1.call-done = bf16[144,576]{1,0:T(8,128)(2,1)} async-done(((bf16[576,576]{1,0:T(8,128)(2,1)}), bf16[144,576]{1,0:T(8,128)(2,1)}) %reduce-scatter.32.cloned.1.call-update) | async-done | bytes 165904 | tf_op jit(solution)/shard_map/reduce_scatter | solution.py:470
  1140.3 22.0 %reduce-scatter.18.cloned.1.call-done = bf16[64,576]{1,0:T(8,128)(2,1)} async-done(((bf16[256,576]{1,0:T(8,128)(2,1)}), bf16[64,576]{1,0:T(8,128)(2,1)}) %reduce-scatter.18.cloned.1.call-update) | async-done | bytes 73744 | tf_op jit(solution)/shard_map/reduce_scatter | solution.py:257
  1165.2 42.1 %all-reduce.8.cloned.1.call-done = (bf16[1,144]{1,0:T(2,128)(2,1)}, bf16[1,144,192]{2,1,0:T(8,128)(2,1)}, bf16[1,144,192]{2,1,0:T(8,128)(2,1)}, bf16[1,144]{1,0:T(2,128)(2,1)}) async-done(((bf16[1,144]{1,0:T(2,128)(2,1)}, bf16[1,144,192]{2,1,0:T(8,128)(2,1)}, bf16[1,144,192]{2,1,0:T(8,128)(2,1)}, bf16[1,144]{1,0:T(2,128)(2,1)}), (bf16[1,144]{1,0:T(2,128)(2,1)}, bf16[1,144,192]{2,1,0:T(8,128)(2,1)}, ...) | async-done | bytes 111184 | tf_op jit(solution)/shard_map/psum | solution.py:505
  1207.3 1.6 broadcast_in_dim.396
  1208.9 1.6 broadcast_in_dim.398
  1212.8 61.8 %all-reduce.10.cloned.1.call-done = (bf16[1,144,576]{2,1,0:T(8,128)(2,1)}, bf16[1,144,576]{2,1,0:T(8,128)(2,1)}, bf16[1,576,384]{2,1,0:T(8,128)(2,1)}, bf16[1,576,384]{2,1,0:T(8,128)(2,1)}, bf16[1,384,576]{1,2,0:T(8,128)(2,1)}) async-done(((bf16[1,144,576]{2,1,0:T(8,128)(2,1)}, bf16[1,144,576]{2,1,0:T(8,128)(2,1)}, bf16[1,576,384]{2,1,0:T(8,128)(2,1)}, bf16[1,576,384]{2,1,0:T(8,128)(2,1)}, ...) | async-done | bytes 1658896 | tf_op jit(solution)/shard_map/psum | solution.py:501
  1274.6 2.1 broadcast_in_dim.408
  (1318 shorter events, 298.0 us)
Async XLA Ops:
  7.2 137.6 %copy-start = (bf16[1,576,384]{2,1,0:T(8,128)(2,1)S(1)}, bf16[1,576,384]{2,1,0:T(8,128)(2,1)}, u32[]{:S(2)}) copy-start(bf16[1,576,384]{2,1,0:T(8,128)(2,1)} %param.33) | copy-start | bytes 1327108
  7.2 96.9 %all-gather.8.cloned.1.call-start = ((), (), s32[]{:S(2)}) async-start(), calls=%async_computation.13 | async-start | bytes 1671168 | tf_op jit(solution)/shard_map/all_gather | solution.py:186
  9.6 52.2 %copy-start.160 = (f32[64,64]{0,1:T(8,128)}, f32[64,64]{0,1:T(8,128)S(1)}, u32[]{:S(2)}) copy-start(f32[64,64]{0,1:T(8,128)S(1)} %pad_maximum_fusion.7) | copy-start | bytes 49156
  10.6 31.5 %copy-start.271 = (f32[64]{0:T(128)}, f32[64]{0:T(128)S(1)}, u32[]{:S(2)}) copy-start(f32[64]{0:T(128)S(1)} %fusion.256) | copy-start | bytes 772
  10.6 50.5 %copy-start.254 = (f32[64]{0:T(128)}, f32[64]{0:T(128)S(1)}, u32[]{:S(2)}) copy-start(f32[64]{0:T(128)S(1)} %add_rsqrt_fusion.5) | copy-start | bytes 772
  26.7 34.5 %copy-start.152 = (f32[576]{0:T(1024)}, f32[576]{0:T(1024)S(1)}, u32[]{:S(2)}) copy-start(f32[576]{0:T(1024)S(1)} %reduce) | copy-start | bytes 6916
  27.1 34.7 %copy-start.150 = (f32[64,64]{0,1:T(8,128)}, f32[64,64]{0,1:T(8,128)S(1)}, u32[]{:S(2)}) copy-start(f32[64,64]{0,1:T(8,128)S(1)} %get-tuple-element.1125) | copy-start | bytes 49156
  27.1 164.7 %copy-start.120 = (f32[64,64]{0,1:T(8,128)}, f32[64,64]{0,1:T(8,128)S(1)}, u32[]{:S(2)}) copy-start(f32[64,64]{0,1:T(8,128)S(1)} %get-tuple-element.1126) | copy-start | bytes 49156
  43.3 124.5 %reduce-scatter.14.cloned.1.call-start = ((), (), s32[]{:S(2)}) async-start(), calls=%async_computation.14 | async-start | bytes 409600 | tf_op jit(solution)/shard_map/reduce_scatter | solution.py:257
  60.8 264.5 %copy-start.2 = (bf16[1,576,576]{2,1,0:T(8,128)(2,1)}, bf16[1,576,576]{2,1,0:T(8,128)(2,1)S(1)}, u32[]{:S(2)}) copy-start(bf16[1,576,576]{2,1,0:T(8,128)(2,1)S(1)} %all-gather.2) | copy-start | bytes 1990660
  62.6 66.7 %copy-start.196 = (f32[576]{0:T(1024)}, f32[576]{0:T(1024)S(1)}, u32[]{:S(2)}) copy-start(f32[576]{0:T(1024)S(1)} %reduce.1) | copy-start | bytes 6916
  129.2 38.5 %copy-start.103 = (f32[64,576]{1,0:T(8,128)}, f32[64,576]{1,0:T(8,128)S(1)}, u32[]{:S(2)}) copy-start(f32[64,576]{1,0:T(8,128)S(1)} %get-tuple-element.1102) | copy-start | bytes 442372
  145.9 32.9 %copy-start.56 = (bf16[2,256,384]{2,1,0:T(8,128)(2,1)}, bf16[2,256,384]{2,1,0:T(8,128)(2,1)S(1)}, u32[]{:S(2)}) copy-start(bf16[2,256,384]{2,1,0:T(8,128)(2,1)S(1)} %get-tuple-element.986) | copy-start | bytes 1179652
  145.9 21.0 %copy-start.25 = (f32[3,3,64,64]{3,2,1,0:T(8,128)S(1)}, f32[3,3,64,64]{3,2,1,0:T(8,128)}, u32[]{:S(2)}) copy-start(f32[3,3,64,64]{3,2,1,0:T(8,128)} %get-tuple-element.362) | copy-start | bytes 442372
  145.9 21.0 %copy-start.201 = (f32[3,3,64]{2,1,0:T(4,128)S(1)}, f32[3,3,64]{2,1,0:T(4,128)}, u32[]{:S(2)}) copy-start(f32[3,3,64]{2,1,0:T(4,128)} %copy-done.200) | copy-start | bytes 6916
  147.1 86.3 %all-gather.10.cloned.1.call-start = ((), (), s32[]{:S(2)}) async-start(), calls=%async_computation.15 | async-start | bytes 1671168 | tf_op jit(solution)/shard_map/all_gather | solution.py:186
  169.3 2.9 collective-permute-start
  177.9 128.4 %reduce-scatter.16.cloned.1.call-start = ((), (), s32[]{:S(2)}) async-start(), calls=%async_computation.16 | async-start | bytes 409600 | tf_op jit(solution)/shard_map/reduce_scatter | solution.py:257
  233.9 34.5 %copy-start.67 = (bf16[64,576]{1,0:T(8,128)(2,1)S(1)}, bf16[64,576]{1,0:T(8,128)(2,1)}, u32[]{:S(2)}) copy-start(bf16[64,576]{1,0:T(8,128)(2,1)} %copy-done.66) | copy-start | bytes 221188
  268.7 20.9 %copy-start.109 = (f32[64,576]{1,0:T(8,128)}, f32[64,576]{1,0:T(8,128)S(1)}, u32[]{:S(2)}) copy-start(f32[64,576]{1,0:T(8,128)S(1)} %get-tuple-element.1105) | copy-start | bytes 442372
  287.3 82.6 %all-gather.12.cloned.1.call-start = ((), (), s32[]{:S(2)}) async-start(), calls=%async_computation.17 | async-start | bytes 1671168 | tf_op jit(solution)/shard_map/all_gather | solution.py:186
  289.7 25.0 %copy-start.39 = (f32[2,64,576]{2,1,0:T(8,128)}, f32[2,64,576]{2,1,0:T(8,128)S(1)}, u32[]{:S(2)}) copy-start(f32[2,64,576]{2,1,0:T(8,128)S(1)} %bitcast_dynamic-update-slice_fusion.16) | copy-start | bytes 884740
  289.7 20.9 %copy-start.19 = (bf16[1,576,192]{2,1,0:T(8,128)(2,1)S(1)}, bf16[1,576,192]{2,1,0:T(8,128)(2,1)}, u32[]{:S(2)}) copy-start(bf16[1,576,192]{2,1,0:T(8,128)(2,1)} %copy-done.17) | copy-start | bytes 663556
  289.7 20.9 %copy-start.154 = (f32[576]{0:T(1024)S(1)}, f32[576]{0:T(1024)}, u32[]{:S(2)}) copy-start(f32[576]{0:T(1024)} %copy-done.152) | copy-start | bytes 6916
  289.8 21.7 %copy-start.30 = (bf16[1,576,192]{2,1,0:T(8,128)(2,1)S(1)}, bf16[1,576,192]{2,1,0:T(8,128)(2,1)}, u32[]{:S(2)}) copy-start(bf16[1,576,192]{2,1,0:T(8,128)(2,1)} %copy-done.28) | copy-start | bytes 663556
  290.6 22.1 %copy-start.148 = (f32[64,64]{0,1:T(8,128)S(1)}, f32[64,64]{0,1:T(8,128)}, u32[]{:S(2)}) copy-start(f32[64,64]{0,1:T(8,128)} %get-tuple-element.1128) | copy-start | bytes 49156
  307.9 1.7 collective-permute-start.1
  310.6 94.5 %copy-start.63 = (bf16[64,576]{1,0:T(8,128)(2,1)}, bf16[64,576]{1,0:T(8,128)(2,1)S(1)}, u32[]{:S(2)}) copy-start(bf16[64,576]{1,0:T(8,128)(2,1)S(1)} %get-tuple-element.997) | copy-start | bytes 221188
  314.6 131.7 %reduce-scatter.20.cloned.1.call-start = ((), (), s32[]{:S(2)}) async-start(), calls=%async_computation.19 | async-start | bytes 409600 | tf_op jit(solution)/shard_map/reduce_scatter | solution.py:342
  326.2 44.3 %copy-start.34 = (f32[3,3,64,64]{3,2,1,0:T(8,128)S(1)}, f32[3,3,64,64]{3,2,1,0:T(8,128)}, u32[]{:S(2)}) copy-start(f32[3,3,64,64]{3,2,1,0:T(8,128)} %custom-call.8) | copy-start | bytes 442372
  405.1 26.9 %copy-start.134 = (bf16[1,64,576]{1,2,0:T(8,128)(2,1)}, bf16[1,64,576]{1,2,0:T(8,128)(2,1)S(1)}, u32[]{:S(2)}) copy-start(bf16[1,64,576]{1,2,0:T(8,128)(2,1)S(1)} %get-tuple-element.1045) | copy-start | bytes 221188
  405.5 26.7 %copy-start.107 = (f32[64,576]{1,0:T(8,128)}, f32[64,576]{1,0:T(8,128)S(1)}, u32[]{:S(2)}) copy-start(f32[64,576]{1,0:T(8,128)S(1)} %get-tuple-element.1108) | copy-start | bytes 442372
  427.4 189.1 %reduce-scatter.22.cloned.1.call-start = ((), (), s32[]{:S(2)}) async-start(), calls=%async_computation.20 | async-start | bytes 3342336 | tf_op jit(solution)/shard_map/reduce_scatter | solution.py:426
  485.7 175.1 %reduce-scatter.24.cloned.1.call-start = ((), (), s32[]{:S(2)}) async-start(), calls=%async_computation.21 | async-start | bytes 409600 | tf_op jit(solution)/shard_map/reduce_scatter | solution.py:342
  489.6 131.7 %copy-start.44 = (f32[2,64,576]{2,1,0:T(8,128)}, f32[2,64,576]{2,1,0:T(8,128)S(1)}, u32[]{:S(2)}) copy-start(f32[2,64,576]{2,1,0:T(8,128)S(1)} %fusion.238) | copy-start | bytes 884740
  489.7 128.5 %copy-start.31 = (bf16[1,576,192]{2,1,0:T(8,128)(2,1)S(1)}, bf16[1,576,192]{2,1,0:T(8,128)(2,1)}, u32[]{:S(2)}) copy-start(bf16[1,576,192]{2,1,0:T(8,128)(2,1)} %copy-done.28) | copy-start | bytes 663556
  491.1 127.7 %copy-start.20 = (bf16[1,576,192]{2,1,0:T(8,128)(2,1)S(1)}, bf16[1,576,192]{2,1,0:T(8,128)(2,1)}, u32[]{:S(2)}) copy-start(bf16[1,576,192]{2,1,0:T(8,128)(2,1)} %copy-done.17) | copy-start | bytes 663556
  622.1 1.3 collective-permute-start.2
  639.7 21.1 %copy-start.42 = (f32[2,64,576]{2,1,0:T(8,128)S(1)}, f32[2,64,576]{2,1,0:T(8,128)}, u32[]{:S(2)}) copy-start(f32[2,64,576]{2,1,0:T(8,128)} %copy-done.41) | copy-start | bytes 884740
  639.7 22.6 %copy-start.268 = (f32[64]{0:T(128)S(1)}, f32[64]{0:T(128)}, u32[]{:S(2)}) copy-start(f32[64]{0:T(128)} %get-tuple-element.1089) | copy-start | bytes 772
  640.9 195.8 %reduce-scatter.26.cloned.1.call-start = ((), (), s32[]{:S(2)}) async-start(), calls=%async_computation.22 | async-start | bytes 3342336 | tf_op jit(solution)/shard_map/reduce_scatter | solution.py:426
  705.9 173.8 %reduce-scatter.28.cloned.1.call-start = ((), (), s32[]{:S(2)}) async-start(), calls=%async_computation.23 | async-start | bytes 409600 | tf_op jit(solution)/shard_map/reduce_scatter | solution.py:342
  709.5 128.1 %copy-start.144 = (f32[128,384]{1,0:T(8,128)S(1)}, f32[128,384]{1,0:T(8,128)}, u32[]{:S(2)}) copy-start(f32[128,384]{1,0:T(8,128)} %copy-done.143) | copy-start | bytes 589828
  711.3 126.5 %copy-start.32 = (bf16[1,576,192]{2,1,0:T(8,128)(2,1)S(1)}, bf16[1,576,192]{2,1,0:T(8,128)(2,1)}, u32[]{:S(2)}) copy-start(bf16[1,576,192]{2,1,0:T(8,128)(2,1)} %copy-done.28) | copy-start | bytes 663556
  841.3 1.3 collective-permute-start.3
  858.8 20.9 %copy-start.43 = (f32[2,64,576]{2,1,0:T(8,128)S(1)}, f32[2,64,576]{2,1,0:T(8,128)}, u32[]{:S(2)}) copy-start(f32[2,64,576]{2,1,0:T(8,128)} %copy-done.41) | copy-start | bytes 884740
  858.8 22.0 %copy-start.265 = (f32[64]{0:T(128)S(1)}, f32[64]{0:T(128)}, u32[]{:S(2)}) copy-start(f32[64]{0:T(128)} %get-tuple-element.1088) | copy-start | bytes 772
  860.0 185.9 %reduce-scatter.30.cloned.1.call-start = ((), (), s32[]{:S(2)}) async-start(), calls=%async_computation.24 | async-start | bytes 3342336 | tf_op jit(solution)/shard_map/reduce_scatter | solution.py:426
  915.4 167.5 %reduce-scatter.36.cloned.1.call-start = ((), (), s32[]{:S(2)}) async-start(), calls=%async_computation.27 | async-start | bytes 368640 | tf_op jit(solution)/shard_map/reduce_scatter | solution.py:476
  921.4 125.4 %copy-start.175 = (f32[2,64,384]{2,1,0:T(8,128)S(1)}, f32[2,64,384]{2,1,0:T(8,128)}, u32[]{:S(2)}) copy-start(f32[2,64,384]{2,1,0:T(8,128)} %copy-done.174) | copy-start | bytes 589828
  921.4 125.5 %copy-start.33 = (bf16[1,576,192]{2,1,0:T(8,128)(2,1)S(1)}, bf16[1,576,192]{2,1,0:T(8,128)(2,1)}, u32[]{:S(2)}) copy-start(bf16[1,576,192]{2,1,0:T(8,128)(2,1)} %copy-done.28) | copy-start | bytes 663556
  924.2 123.3 %copy-start.22 = (bf16[1,576,192]{2,1,0:T(8,128)(2,1)S(1)}, bf16[1,576,192]{2,1,0:T(8,128)(2,1)}, u32[]{:S(2)}) copy-start(bf16[1,576,192]{2,1,0:T(8,128)(2,1)} %copy-done.17) | copy-start | bytes 663556
  1051.5 40.0 %reduce-scatter.34.cloned.1.call-start = ((), (), s32[]{:S(2)}) async-start(), calls=%async_computation.26 | async-start | bytes 368640 | tf_op jit(solution)/shard_map/reduce_scatter | solution.py:473
  1052.7 62.2 %reduce-scatter.38.cloned.1.call-start = ((), (), s32[]{:S(2)}) async-start(), calls=%async_computation.28 | async-start | bytes 921600 | tf_op jit(solution)/shard_map/reduce_scatter | solution.py:479
  1055.4 84.5 %reduce-scatter.32.cloned.1.call-start = ((), (), s32[]{:S(2)}) async-start(), calls=%async_computation.25 | async-start | bytes 921600 | tf_op jit(solution)/shard_map/reduce_scatter | solution.py:470
  1059.8 102.4 %reduce-scatter.18.cloned.1.call-start = ((), (), s32[]{:S(2)}) async-start(), calls=%async_computation.18 | async-start | bytes 409600 | tf_op jit(solution)/shard_map/reduce_scatter | solution.py:257
  1065.1 142.3 %all-reduce.8.cloned.1.call-start = ((), (), s32[]{:S(2)}) async-start(), calls=%async_computation.29 | async-start | bytes 299008 | tf_op jit(solution)/shard_map/psum | solution.py:505
  1069.8 21.7 %copy-start.139 = (bf16[256,576]{1,0:T(8,128)(2,1)S(1)}, bf16[256,576]{1,0:T(8,128)(2,1)}, u32[]{:S(2)}) copy-start(bf16[256,576]{1,0:T(8,128)(2,1)} %copy-done.138) | copy-start | bytes 884740
  1091.5 183.0 %all-reduce.10.cloned.1.call-start = ((), (), s32[]{:S(2)}) async-start(), calls=%async_computation.30 | async-start | bytes 3391488 | tf_op jit(solution)/shard_map/psum | solution.py:501
  1092.7 47.2 %copy-start.205 = (bf16[1,64,576]{2,1,0:T(8,128)(2,1)S(1)}, bf16[1,64,576]{2,1,0:T(8,128)(2,1)}, u32[]{:S(2)}) copy-start(bf16[1,64,576]{2,1,0:T(8,128)(2,1)} %get-tuple-element.998) | copy-start | bytes 221188
  1092.7 47.4 %copy-start.93 = (bf16[2,64,576]{1,2,0:T(8,128)(2,1)S(1)}, bf16[2,64,576]{1,2,0:T(8,128)(2,1)}, u32[]{:S(2)}) copy-start(bf16[2,64,576]{1,2,0:T(8,128)(2,1)} %copy-done.92) | copy-start | bytes 442372
  1139.9 22.4 %copy-start.108 = (f32[64,576]{1,0:T(8,128)S(1)}, f32[64,576]{1,0:T(8,128)}, u32[]{:S(2)}) copy-start(f32[64,576]{1,0:T(8,128)} %copy-done.107) | copy-start | bytes 442372
  1140.0 24.3 %copy-start.208 = (bf16[1,1,64,576]{3,2,1,0:T(8,128)(2,1)S(1)}, bf16[1,1,64,576]{3,2,1,0:T(8,128)(2,1)}, u32[]{:S(2)}) copy-start(bf16[1,1,64,576]{3,2,1,0:T(8,128)(2,1)} %get-tuple-element.1083) | copy-start | bytes 221188
  1140.1 24.2 %copy-start.97 = (bf16[2,64,576]{1,2,0:T(8,128)(2,1)S(1)}, bf16[2,64,576]{1,2,0:T(8,128)(2,1)}, u32[]{:S(2)}) copy-start(bf16[2,64,576]{1,2,0:T(8,128)(2,1)} %copy-done.96) | copy-start | bytes 442372
  (298 other events, 1141.6 us)
Sparse Core Ops, SparseCore 0:
  43.4 60.7 all-gather.7
  147.2 19.6 reduce-scatter.13
  178.0 55.2 all-gather.9
  287.5 18.7 reduce-scatter.15
  314.7 55.1 all-gather.11
  427.5 18.7 reduce-scatter.19
  485.8 130.5 reduce-scatter.21
  641.0 19.7 reduce-scatter.23
  706.0 130.5 reduce-scatter.25
  860.1 19.5 reduce-scatter.27
  915.5 130.3 reduce-scatter.29
  1051.6 19.1 reduce-scatter.35
  1073.0 18.4 reduce-scatter.33
  1093.7 21.2 reduce-scatter.37
  1117.7 22.1 reduce-scatter.31
  1142.6 19.6 reduce-scatter.17
  1165.9 41.3 all-reduce.7
  1211.4 63.1 all-reduce.9
where the time goes:
time: 1300 us; the launch traced here: 1290 us
  waiting for transfers between devices  725 us (56%)
  local copies, waits for them, and re-layouts  168 us (13%)
  blocking collectives  167 us (13%)
  matrix products  98.7 us (8%)
  other arithmetic  91.8 us (7%)
  between operations  19.1 us (1%)
  loops' own time  17.5 us (1%)
    reduce_scatter x3, waiting for transfers between devices, local(): lax.psum_scatter(key_terms, ('ctx', 'wt'), scatter_dimension=0, tiled=True)  371 us
    all_gather x3, waiting for transfers between devices, local(): lax.all_gather(layer_kv_cache.reshape(local_keys, 2 * key_value_width), (...  106 us
    psum x1, waiting for transfers between devices, local(): lax.psum(share_query.astype(jnp.bfloat16), 'ctx').astype(jnp.float32)  61.8 us
    reduce_scatter x3, waiting for transfers between devices, local(): lax.psum_scatter(mlp_term.astype(jnp.bfloat16), 'wt', scatter_dimension=0...  47.9 us
    all_gather x3, blocking collectives, local(): out_rows = lax.all_gather(out_grad, 'wt', axis=0, tiled=True)  45.1 us
    all_gather x3, blocking collectives, local(): layer_mlp_rows = lax.all_gather(mlp_in, 'wt', axis=0, tiled=True)  44.3 us
    psum x1, waiting for transfers between devices, local(): lax.psum(share_gain_attn.astype(jnp.bfloat16), 'ctx').astype(jnp.float32)  42.1 us
    reduce_scatter x3, waiting for transfers between devices, local(): lax.psum_scatter(branch_out.astype(jnp.bfloat16), 'wt', scatter_dimension...  37.7 us
  transfers between devices with their start and end apart: 22, of which 18 were waited for; matrix products, arithmetic and copies ran while one was open for 7% of the time, Pallas kernels for 0%

commit v1 on v0

v1 whole, which is shorter than its diff:
```python
import functools

import jax
import jax.numpy as jnp
from jax import lax
from jax.experimental import pallas as pl
from jax.experimental.pallas import tpu as pltpu
from jax.sharding import PartitionSpec as P

HEADS = 9
KV = 3
GROUP = HEADS // KV
HD = 64
KVW = KV * HD
EPS = 1e-05
THETA = 100000.0
FLOOR = -1e30
BF = jnp.bfloat16
F32 = jnp.float32
VMEM_LIMIT = 60 * 1024 * 1024
MESH = pl.DeviceIdType.MESH

IDS = {}


def group_of(axes, sizes):
    count = 1
    for axis in axes:
        count *= sizes[axis]
    return count


def my_index(axes, sizes):
    index = 0
    for axis in axes:
        index = index * sizes[axis] + lax.axis_index(axis)
    return index


def device_at(axes, index, sizes):
    where = {}
    for axis in reversed(axes):
        where[axis] = lax.rem(index, sizes[axis])
        index = lax.div(index, sizes[axis])
    return where


def comm_kernel(plan, sizes, n_in, *refs):
    n_ops = len(plan)
    ins = refs[:n_in]
    outs = refs[n_in : n_in + n_ops]
    sems = refs[n_in + n_ops :]
    section = lax.axis_index("section")
    partner = {"section": 1 - section}
    groups = []
    swaps = False
    for kind, axes in plan:
        if kind in ("swap2", "agswap", "swap"):
            swaps = True
        if kind in ("ag", "a2a", "agswap") and axes not in groups:
            groups.append(axes)
    barrier = pltpu.get_barrier_semaphore()
    expected = 0
    for axes in groups:
        n = group_of(axes, sizes)
        me = my_index(axes, sizes)
        for d in range(1, n):
            peer = lax.rem(me + d, n)
            pl.semaphore_signal(
                barrier, inc=1, device_id=device_at(axes, peer, sizes), device_id_type=MESH
            )
            expected += 1
    if swaps:
        pl.semaphore_signal(barrier, inc=1, device_id=partner, device_id_type=MESH)
        expected += 1
    pl.semaphore_wait(barrier, expected)

    def remote(src, dst, send, recv, where):
        return pltpu.make_async_remote_copy(
            src_ref=src, dst_ref=dst, send_sem=send, recv_sem=recv, device_id=where,
            device_id_type=MESH,
        )

    pending = []
    forwards = []
    at = 0
    for slot, (kind, axes) in enumerate(plan):
        out = outs[slot]
        send, recv, local, fsend, frecv = sems[5 * slot : 5 * slot + 5]
        if kind == "swap2":
            first, second = ins[at], ins[at + 1]
            at += 2

            @pl.when(section == 0)
            def _():
                remote(second, out, send.at[0], recv.at[0], partner).start()

            @pl.when(section == 1)
            def _():
                remote(first, out, send.at[0], recv.at[0], partner).start()

            pending.append(remote(first, out, send.at[0], recv.at[0], partner))
            continue
        x = ins[at]
        at += 1
        if kind == "swap":
            copy = remote(x.at[1 - section], out, send.at[0], recv.at[0], partner)
            copy.start()
            pending.append(copy)
            continue
        n = group_of(axes, sizes)
        me = my_index(axes, sizes)
        target = out.at[section] if kind == "agswap" else out
        for d in range(1, n):
            peer = lax.rem(me + d, n)
            source = x.at[peer] if kind == "a2a" else x
            remote(
                source, target.at[me], send.at[peer], recv.at[me], device_at(axes, peer, sizes)
            ).start()
        own = pltpu.make_async_copy(x.at[me] if kind == "a2a" else x, target.at[me], local)
        own.start()
        if kind == "agswap":
            forward = remote(x, target.at[me], fsend.at[me], frecv.at[me], partner)
            forward.start()
        forwards.append((kind, axes, x, out, target, own, sems[5 * slot : 5 * slot + 5]))
    for kind, axes, x, out, target, own, (send, recv, local, fsend, frecv) in forwards:
        n = group_of(axes, sizes)
        me = my_index(axes, sizes)
        for d in range(1, n):
            peer = lax.rem(me + n - d, n)
            where = device_at(axes, peer, sizes)
            source = x.at[peer] if kind == "a2a" else x
            copy = remote(source, target.at[peer], send.at[peer], recv.at[peer], where)
            copy.wait_recv()
            if kind == "agswap":
                remote(
                    target.at[peer], target.at[peer], fsend.at[peer], frecv.at[peer], partner
                ).start()
        own.wait()
        for d in range(1, n):
            peer = lax.rem(me + n - d, n)
            where = device_at(axes, peer, sizes)
            source = x.at[peer] if kind == "a2a" else x
            remote(source, target.at[peer], send.at[peer], recv.at[peer], where).wait_send()
        if kind == "agswap":
            other = out.at[1 - section]
            for d in range(n):
                peer = lax.rem(me + n - d, n)
                copy = remote(
                    target.at[peer], other.at[peer], fsend.at[peer], frecv.at[peer], partner
                )
                copy.wait_send()
                copy.wait_recv()
    for copy in pending:
        copy.wait_send()
        copy.wait_recv()


def communicate(sizes, *ops):
    plan, arrays, shapes, scratch = [], [], [], []
    for kind, axes, x in ops:
        plan.append((kind, axes))
        if kind == "swap2":
            arrays.extend(x)
            n, shape, dtype = 1, x[0].shape, x[0].dtype
        else:
            arrays.append(x)
            n, shape, dtype = 1, x.shape, x.dtype
            if kind == "swap":
                shape = x.shape[1:]
            else:
                n = group_of(axes, sizes)
                if kind == "ag":
                    shape = (n,) + x.shape
                elif kind == "agswap":
                    shape = (2, n) + x.shape
        shapes.append(jax.ShapeDtypeStruct(shape, dtype))
        dma = pltpu.SemaphoreType.DMA
        scratch += [dma((n,)), dma((n,)), dma(()), dma((n,)), dma((n,))]
    key = (tuple(plan), tuple((a.shape, str(a.dtype)) for a in arrays))
    ident = IDS.setdefault(key, len(IDS))
    space = pl.BlockSpec(memory_space=pltpu.VMEM)
    out = pl.pallas_call(
        functools.partial(comm_kernel, tuple(plan), sizes, len(arrays)),
        out_shape=shapes,
        in_specs=[space] * len(arrays),
        out_specs=[space] * len(shapes),
        scratch_shapes=scratch,
        compiler_params=pltpu.CompilerParams(
            collective_id=ident, has_side_effects=True, vmem_limit_bytes=VMEM_LIMIT
        ),
        name="comm%d" % ident,
    )(*arrays)
    return out


def nt(a, b):
    return lax.dot_general(a, b, (((1,), (1,)), ((), ())), preferred_element_type=F32)


def tn(a, b):
    return lax.dot_general(a, b, (((0,), (0,)), ((), ())), preferred_element_type=F32)


def nn(a, b):
    return jnp.dot(a, b, preferred_element_type=F32)


def stack_heads(x, g):
    first = g * GROUP * HD
    return jnp.concatenate([x[:, first + i * HD : first + (i + 1) * HD] for i in range(GROUP)], 0)


def attend_kernel(chunk, q_ref, kv_ref, pos_ref, doc_ref, o_ref, lse_ref):
    rows = q_ref.shape[0]
    wide = GROUP * rows
    keys = kv_ref.shape[0]
    q = q_ref[...].astype(F32)
    pos = pos_ref[...]
    doc = doc_ref[...]
    for g in range(KV):
        qg = stack_heads(q, g).astype(BF)

        def step(i, carry, qg=qg, g=g):
            top, total, acc = carry
            base = pl.multiple_of(i * chunk, chunk)
            k = kv_ref[pl.ds(base, chunk), g * HD : (g + 1) * HD]
            v = kv_ref[pl.ds(base, chunk), KVW + g * HD : KVW + (g + 1) * HD]
            s = nt(k, qg) * 0.125
            at = base + lax.broadcasted_iota(jnp.int32, (chunk, wide), 0)
            s = jnp.where((at <= pos) & (at >= doc), s, FLOOR)
            new = jnp.maximum(top, jnp.max(s, 0, keepdims=True))
            scale = jnp.exp(top - new)
            p = jnp.exp(s - new)
            total = total * scale + jnp.sum(p, 0, keepdims=True)
            acc = acc * scale + tn(v, p.astype(BF))
            return new, total, acc

        top, total, acc = lax.fori_loop(
            0,
            keys // chunk,
            step,
            (
                jnp.full((1, wide), FLOOR, F32),
                jnp.zeros((1, wide), F32),
                jnp.zeros((HD, wide), F32),
            ),
        )
        out = jnp.transpose(acc / total)
        for i in range(GROUP):
            h = g * GROUP + i
            o_ref[:, h * HD : (h + 1) * HD] = out[i * rows : (i + 1) * rows, :].astype(BF)
        lse_ref[g : g + 1, :] = top + jnp.log(total)


def attend(q, kv, pos, doc):
    rows = q.shape[0]
    keys = kv.shape[0]
    return pl.pallas_call(
        functools.partial(attend_kernel, 512 if keys % 512 == 0 else keys),
        out_shape=[
            jax.ShapeDtypeStruct(q.shape, BF),
            jax.ShapeDtypeStruct((KV, GROUP * rows), F32),
        ],
        compiler_params=pltpu.CompilerParams(vmem_limit_bytes=VMEM_LIMIT),
        name="attend",
    )(q, kv, pos, doc)


def attend_back_kernel(
    chunk, q_ref, do_ref, o_ref, kv_ref, lse_ref, pos_ref, doc_ref, dq_ref, dkv_ref
):
    rows = q_ref.shape[0]
    wide = GROUP * rows
    keys = kv_ref.shape[0]
    q = q_ref[...].astype(F32)
    do = do_ref[...].astype(F32)
    prod = do * o_ref[...].astype(F32)
    pos = pos_ref[...]
    doc = doc_ref[...]
    for g in range(KV):
        qg = stack_heads(q, g).astype(BF)
        dog = stack_heads(do, g).astype(BF)
        delta = jnp.sum(jnp.transpose(stack_heads(prod, g)), 0, keepdims=True)
        lse = lse_ref[g : g + 1, :]

        def step(i, dq, qg=qg, dog=dog, delta=delta, lse=lse, g=g):
            base = pl.multiple_of(i * chunk, chunk)
            k = kv_ref[pl.ds(base, chunk), g * HD : (g + 1) * HD]
            v = kv_ref[pl.ds(base, chunk), KVW + g * HD : KVW + (g + 1) * HD]
            s = nt(k, qg) * 0.125
            at = base + lax.broadcasted_iota(jnp.int32, (chunk, wide), 0)
            s = jnp.where((at <= pos) & (at >= doc), s, FLOOR)
            p = jnp.exp(s - lse)
            dp = nt(v, dog)
            ds = (p * (dp - delta)).astype(BF)
            dkv_ref[pl.ds(base, chunk), g * HD : (g + 1) * HD] = (nn(ds, qg) * 0.125).astype(BF)
            dkv_ref[pl.ds(base, chunk), KVW + g * HD : KVW + (g + 1) * HD] = nn(
                p.astype(BF), dog
            ).astype(BF)
            return dq + tn(k, ds)

        dq = lax.fori_loop(0, keys // chunk, step, jnp.zeros((HD, wide), F32))
        out = jnp.transpose(dq * 0.125)
        for i in range(GROUP):
            h = g * GROUP + i
            dq_ref[:, h * HD : (h + 1) * HD] = out[i * rows : (i + 1) * rows, :]


def attend_back(q, do, o, kv, lse, pos, doc):
    keys = kv.shape[0]
    return pl.pallas_call(
        functools.partial(attend_back_kernel, 512 if keys % 512 == 0 else keys),
        out_shape=[jax.ShapeDtypeStruct(q.shape, F32), jax.ShapeDtypeStruct(kv.shape, BF)],
        compiler_params=pltpu.CompilerParams(vmem_limit_bytes=VMEM_LIMIT),
        name="attend_back",
    )(q, do, o, kv, lse, pos, doc)


def low_half(width):
    return (jnp.arange(width, dtype=jnp.int32) % HD < HD // 2)[None, :]


def rope(x, cos, sin):
    half = HD // 2
    w = x.shape[1]
    turned = jnp.where(low_half(w), -jnp.roll(x, -half, 1), jnp.roll(x, half, 1))
    return x * cos[:, :w] + turned * sin[:, :w]


def rope_back(x, cos, sin):
    half = HD // 2
    w = x.shape[1]
    scaled = x * sin[:, :w]
    turned = jnp.where(low_half(w), jnp.roll(scaled, -half, 1), -jnp.roll(scaled, half, 1))
    return x * cos[:, :w] + turned


def local(
    sizes, inputs, doc_start, attn_gain, w_q, w_k, w_v, w_o, mlp_gain, w_gate, w_up, w_down,
    cotangent,
):
    micro, rows, width = inputs.shape
    n_ctx, n_wt = sizes["ctx"], sizes["wt"]
    n_place = n_ctx * n_wt
    section = lax.axis_index("section")
    wt = lax.axis_index("wt")
    place = lax.axis_index("ctx") * n_wt + wt
    batch = n_place * rows
    keys = micro * batch
    qw = HEADS * HD
    fused = jnp.concatenate([w_q[0], w_k[0], w_v[0], w_o[0]], 1)
    x_in = lax.dynamic_index_in_dim(inputs, section, 0, keepdims=False)
    cot = lax.dynamic_index_in_dim(cotangent, section, 0, keepdims=False)
    gains = jnp.concatenate([attn_gain, mlp_gain], 0)
    weights, gates, ups, downs, all_gains, cot_rows = communicate(
        sizes,
        ("agswap", ("wt",), fused),
        ("ag", ("section",), w_gate[0]),
        ("ag", ("section",), w_up[0]),
        ("ag", ("section",), w_down[0]),
        ("ag", ("section",), gains),
        ("ag", ("wt",), cot.astype(BF)),
    )
    weights = weights.reshape(2, width, fused.shape[1])
    w_qkv = weights[:, :, : qw + 2 * KVW]
    w_out = weights[:, :, qw + 2 * KVW :]

    pos = section * batch + place * rows + jnp.arange(rows, dtype=jnp.int32)
    doc = lax.dynamic_slice(doc_start, (section, place * rows), (1, rows))[0]
    half = HD // 2
    inverse = 1.0 / THETA ** (jnp.arange(half).astype(F32) * 2.0 / HD)
    angles = (pos - doc).astype(F32)[:, None] * inverse[None, :]
    cos = jnp.tile(jnp.cos(angles), (1, 2 * HEADS))
    sin = jnp.tile(jnp.sin(angles), (1, 2 * HEADS))
    pos_row = jnp.tile(pos, GROUP)[None, :]
    doc_row = jnp.tile(doc, GROUP)[None, :]

    h_in = x_in
    saved = []
    for layer in range(2):
        ga, gm = all_gains[layer, 0], all_gains[layer, 1]
        h = h_in.astype(F32)
        r1 = lax.rsqrt(jnp.mean(h * h, -1, keepdims=True) + EPS)
        n1 = h * r1
        u = (n1 * ga).astype(BF)
        qkv = nn(u, w_qkv[layer])
        q = rope(qkv[:, :qw], cos, sin).astype(BF)
        k = rope(qkv[:, qw : qw + KVW], cos, sin).astype(BF)
        v = qkv[:, qw + KVW :].astype(BF)
        (kv,) = communicate(
            sizes, ("agswap", ("ctx", "wt"), jnp.concatenate([k, v], 1))
        )
        kv = kv.reshape(keys, 2 * KVW)
        o, lse = attend(q, kv, pos_row, doc_row)
        h2 = h + nn(o, w_out[layer])
        r2 = lax.rsqrt(jnp.mean(h2 * h2, -1, keepdims=True) + EPS)
        n2 = h2 * r2
        z = (n2 * gm).astype(BF)
        (zr,) = communicate(sizes, ("ag", ("wt",), z))
        zr = zr.reshape(n_wt * rows, width)
        g = nn(zr, gates[layer])
        up = nn(zr, ups[layer])
        act = (g * jax.nn.sigmoid(g) * up).astype(BF)
        branch = nn(act, downs[layer]).astype(BF).reshape(n_wt, rows, width)
        (parts,) = communicate(sizes, ("a2a", ("wt",), branch))
        out = (h2 + jnp.sum(parts.astype(F32), 0)).astype(BF)
        saved.append((n1, r1, u, q, kv, o, lse, n2, r2, zr, g, up, act))
        h_in = out
        if layer == 0:
            first_out = out
    second_out = h_in

    grads = [None, None]
    e = cot
    er = cot_rows.reshape(n_wt * rows, width)
    for layer in (1, 0):
        ga, gm = all_gains[layer, 0], all_gains[layer, 1]
        n1, r1, u, q, kv, o, lse, n2, r2, zr, g, up, act = saved[layer]
        if layer == 0:
            (er,) = communicate(sizes, ("ag", ("wt",), e))
            er = er.reshape(n_wt * rows, width)
            e = e.astype(F32)
        g_down = tn(act, er)
        da = nt(er, downs[layer])
        s = jax.nn.sigmoid(g)
        dg = (da * up * s * (1.0 + g * (1.0 - s))).astype(BF)
        du = (da * g * s).astype(BF)
        g_gate = tn(zr, dg)
        g_up = tn(zr, du)
        term = (nt(dg, gates[layer]) + nt(du, ups[layer])).astype(BF).reshape(n_wt, rows, width)
        (parts,) = communicate(sizes, ("a2a", ("wt",), term))
        dz = jnp.sum(parts.astype(F32), 0)
        g_gm = jnp.sum(dz * n2, 0)
        m2 = dz * gm
        dh2 = e + r2 * (m2 - n2 * jnp.mean(m2 * n2, -1, keepdims=True))
        ob = dh2.astype(BF)
        g_o = tn(o, ob)
        do = nt(ob, w_out[layer]).astype(BF)
        dq, dkv = attend_back(q, do, o, kv, lse, pos_row, doc_row)
        dkv = dkv.reshape(micro, n_place, rows, 2 * KVW)
        (theirs,) = communicate(sizes, ("swap", (), dkv))
        mine = lax.dynamic_index_in_dim(dkv, section, 0, keepdims=False)
        both = (mine.astype(F32) + theirs.astype(F32)).astype(BF)
        (pieces,) = communicate(sizes, ("a2a", ("ctx", "wt"), both))
        dkv_own = jnp.sum(pieces.astype(F32), 0)
        dqr = rope_back(dq, cos, sin).astype(BF)
        dkr = rope_back(dkv_own[:, :KVW], cos, sin).astype(BF)
        dvr = dkv_own[:, KVW:].astype(BF)
        dqkv = jnp.concatenate([dqr, dkr, dvr], 1)
        g_qkv = tn(u, dqkv)
        du_in = nt(dqkv, w_qkv[layer])
        g_ga = jnp.sum(du_in * n1, 0)
        m1 = du_in * ga
        e = (dh2 + r1 * (m1 - n1 * jnp.mean(m1 * n1, -1, keepdims=True))).astype(BF)
        grads[layer] = (
            jnp.concatenate([g_qkv, g_o], 1).astype(BF),
            g_gate.astype(BF),
            g_up.astype(BF),
            g_down.astype(BF),
            jnp.stack([g_ga, g_gm]),
        )
        if layer == 1:
            second_grad = e
    first_grad = e

    received = communicate(
        sizes,
        ("swap2", (), (first_out, second_out)),
        ("swap2", (), (first_grad, second_grad)),
        *[("swap2", (), pair) for pair in zip(grads[0], grads[1])],
    )

    def keep(pair):
        return jnp.where(section == 0, pair[0], pair[1])

    def whole(own, other):
        return jnp.where(section == 0, jnp.stack([own, other]), jnp.stack([other, own]))

    acts = whole(keep((first_out, second_out)), received[0])
    dacts = whole(keep((first_grad, second_grad)), received[1])
    summed = [
        keep(pair).astype(F32) + other.astype(F32)
        for pair, other in zip(zip(grads[0], grads[1]), received[2:])
    ]
    g_attn, g_gate, g_up, g_down, g_gain = summed
    cols = g_attn.shape[1]
    split = width // n_wt // n_ctx
    g_attn = (
        g_attn.astype(BF).reshape(n_wt, n_ctx, split, cols).transpose(1, 0, 2, 3)
    )
    hidden = g_gate.shape[1]
    r_attn, r_gate, r_up, r_down, r_gain = communicate(
        sizes,
        ("a2a", ("ctx",), g_attn),
        ("a2a", ("ctx",), g_gate.astype(BF).reshape(n_ctx, width // n_ctx, hidden)),
        ("a2a", ("ctx",), g_up.astype(BF).reshape(n_ctx, width // n_ctx, hidden)),
        ("a2a", ("ctx",), g_down.astype(BF).reshape(n_ctx, hidden // n_ctx, width)),
        ("ag", ("ctx", "wt"), g_gain),
    )

    def total(x):
        return jnp.sum(x.astype(F32), 0)

    (p_attn,) = communicate(sizes, ("a2a", ("wt",), total(r_attn).astype(BF)))
    f_attn, f_gate, f_up, f_down = communicate(
        sizes,
        ("ag", ("ctx",), total(p_attn).astype(BF)),
        ("ag", ("ctx",), total(r_gate).astype(BF)),
        ("ag", ("ctx",), total(r_up).astype(BF)),
        ("ag", ("ctx",), total(r_down).astype(BF)),
    )
    f_attn = f_attn.reshape(width // n_wt, cols).astype(F32)
    gain = lax.dynamic_slice_in_dim(total(r_gain), wt * (width // n_wt), width // n_wt, 1)
    return (
        acts[None],
        dacts[None],
        gain[0][None],
        f_attn[None, :, :qw],
        f_attn[None, :, qw : qw + KVW],
        f_attn[None, :, qw + KVW : qw + 2 * KVW],
        f_attn[None, :, qw + 2 * KVW :],
        gain[1][None],
        f_gate.reshape(1, width, hidden).astype(F32),
        f_up.reshape(1, width, hidden).astype(F32),
        f_down.reshape(1, hidden, width).astype(F32),
    )


def solution(mesh):
    in_specs = (
        P(None, ("ctx", "wt"), None),
        P(),
        P("section", None),
        P("section", "wt", None),
        P("section", "wt", None),
        P("section", "wt", None),
        P("section", "wt", None),
        P("section", None),
        P("section", None, "wt"),
        P("section", None, "wt"),
        P("section", "wt", None),
        P(None, ("ctx", "wt"), None),
    )
    out_specs = (
        P("section", None, ("ctx", "wt"), None),
        P("section", None, ("ctx", "wt"), None),
        P("section", "wt"),
        P("section", "wt", None),
        P("section", "wt", None),
        P("section", "wt", None),
        P("section", "wt", None),
        P("section", "wt"),
        P("section", None, "wt"),
        P("section", None, "wt"),
        P("section", "wt", None),
    )
    IDS.clear()
    sizes = dict(mesh.shape)
    return jax.shard_map(
        functools.partial(local, sizes), mesh=mesh, in_specs=in_specs, out_specs=out_specs,
        check_vma=False,
    )
```

time: 1300 us -> 501 us (0.39)
  waiting for transfers between devices: 725 us -> 0 us
  Pallas kernels: 0 us -> 383 us
  blocking collectives: 167 us -> 0 us
  local copies, waits for them, and re-layouts: 168 us -> 23.9 us
  matrix products: 98.7 us -> 40.2 us
  other arithmetic: 91.8 us -> 49.6 us
  loops' own time: 17.5 us -> 0 us
  between operations: 19.1 us -> 1.64 us
    reduce_scatter x13 -> x0, waiting for transfers between devices: 512 us -> none  [the longest x3 371 us: local(): lax.psum_scatter(key_terms, ('ctx', 'wt'), scatter_dimension=0, tiled=True)]
    pallas_call x0 -> x22, Pallas kernels: none -> 383 us  [the longest x18 343 us: communicate(): pl.pallas_call(functools.partial(comm_kernel, tuple(plan), sizes, len(arr...]
    all_gather x10 -> x0, blocking collectives: 156 us -> none  [the longest x3 45.1 us: local(): out_rows = lax.all_gather(out_grad, 'wt', axis=0, tiled=True)]
    all_gather x3 -> x0, waiting for transfers between devices: 106 us -> none  [local(): lax.all_gather(layer_kv_cache.reshape(local_keys, 2 * key_value_width), (...]
    psum x2 -> x0, waiting for transfers between devices: 104 us -> none  [the longest x1 61.8 us: local(): lax.psum(share_query.astype(jnp.bfloat16), 'ctx').astype(jnp.float32)]
    dynamic_slice x79 -> x0, local copies, waits for them, and re-layouts: 61.7 us -> none  [the longest x24 22 us: local(): lax.scan(fold_block, start_state, jnp.arange(whole_keys // block_of_keys))]
    dot_general x147 -> x30, matrix products: 98.7 us -> 40.2 us  [the longest x10 15.6 us: nn(): return jnp.dot(a, b, preferred_element_type=F32)]
    slice x28 -> x20, local copies, waits for them, and re-layouts: 25.5 us -> 2.84 us  [the longest x1 0.8 us: local(): ga, gm = (all_gains[layer, 0], all_gains[layer, 1])]
  transfers between devices with their start and end apart: 22 -> 0, of which waited for: 18 -> 0; matrix products, arithmetic and copies ran while one was open for 7% -> 0% of each run, Pallas kernels for 0% -> 0%
where the time goes in v1:
time: 501 us; the launch traced here: 499 us
  Pallas kernels  383 us (76%)
  other arithmetic  49.6 us (10%)
  matrix products  40.2 us (8%)
  local copies, waits for them, and re-layouts  23.9 us (5%)
    pallas_call x18, Pallas kernels, communicate(): pl.pallas_call(functools.partial(comm_kernel, tuple(plan), sizes, len(arr...  343 us
    pallas_call x2, Pallas kernels, attend_back(): pl.pallas_call(functools.partial(attend_back_kernel, 512 if keys % 512 ==...  21.4 us
    pallas_call x2, Pallas kernels, attend(): pl.pallas_call(functools.partial(attend_kernel, 512 if keys % 512 == 0 el...  18.8 us
    dot_general x10, matrix products, nn(): return jnp.dot(a, b, preferred_element_type=F32)  15.6 us
    dot_general x10, matrix products, nt(): lax.dot_general(a, b, (((1,), (1,)), ((), ())), preferred_element_type=F32)  14.9 us

profile of v1, /device:TPU:0, one launch (start us, length us, event | category | flops | bytes accessed | tf_op | source)
XLA Modules:
  0.0 498.6 jit_solution(15474231887300228720)
XLA Ops:
  0.7 1.6 bitcast_convert_fusion.3.refs_5_
  2.2 2.0 copy.31
  4.3 2.1 concatenate.106.refs_0_
  6.9 54.6 %comm0.1 = (bf16[2,4,144,1536]{3,2,1,0:T(8,128)(2,1)}, bf16[2,576,384]{2,1,0:T(8,128)(2,1)}, bf16[2,576,384]{2,1,0:T(8,128)(2,1)}, bf16[2,384,576]{2,1,0:T(8,128...) custom-call(bf16[144,1536]{1,0:T(8,128)(2,1)} %concatenate.106.refs_0_, bf16[576,384]{1,0:T(8,128)(2,1)} %bitcast.229, ...), custom_call_target="tpu_custom_call" | custom-call | tf_op jit(solution)/shard_map/comm0/pallas_call | solution.py:183
  62.5 1.7 fusion.5
  66.5 26.1 %comm1.2 = bf16[2,16,64,384]{3,2,1,0:T(8,128)(2,1)} custom-call(bf16[64,384]{1,0:T(8,128)(2,1)} %pad_maximum_fusion.4.refs_0_), custom_call_target="tpu_custom_call" | custom-call | tf_op jit(solution)/shard_map/comm1/pallas_call | solution.py:183
  94.8 9.4 %attend.2 = (bf16[64,576]{1,0:T(8,128)(2,1)}, f32[3,192]{1,0:T(4,128)}) custom-call(bf16[64,576]{1,0:T(8,128)(2,1)} %fusion.71.q_ref, bf16[2048,384]{1,0:T(8,128)(2,1)} %bitcast.191, s32[1,192]{1,0:T(1,128)} %broadcast_in_dim_tile.6.pos_ref, s32[1,192]{1,0:T(1,128)} %broadcast_in_dim_tile.7.doc_ref), custom_call_target="tpu_custom_call" | custom-call | tf_op jit(solution)/shard_map/attend/pallas_call | solution.py:259
  104.2 1.8 multiply_reduce_fusion.5
  106.7 11.8 %comm2.3 = bf16[4,64,576]{2,1,0:T(8,128)(2,1)} custom-call(bf16[64,576]{1,0:T(8,128)(2,1)} %multiply_convert_fusion.7.refs_0_), custom_call_target="tpu_custom_call" | custom-call | tf_op jit(solution)/shard_map/comm2/pallas_call | solution.py:183
  118.6 1.4 fusion.26
  120.0 2.2 multiply_convert_fusion.5
  123.5 12.5 %comm3.4 = bf16[4,64,576]{2,1,0:T(8,128)(2,1)} custom-call(bf16[4,64,576]{2,1,0:T(8,128)(2,1)} %bitcast.222), custom_call_target="tpu_custom_call" | custom-call | tf_op jit(solution)/shard_map/comm3/pallas_call | solution.py:183
  137.1 1.7 fusion.7
  139.9 25.1 %comm1.3 = bf16[2,16,64,384]{3,2,1,0:T(8,128)(2,1)} custom-call(bf16[64,384]{1,0:T(8,128)(2,1)} %pad_maximum_fusion.5.refs_0_), custom_call_target="tpu_custom_call" | custom-call | tf_op jit(solution)/shard_map/comm1/pallas_call | solution.py:183
  165.9 9.4 %attend.3 = (bf16[64,576]{1,0:T(8,128)(2,1)}, f32[3,192]{1,0:T(4,128)}) custom-call(bf16[64,576]{1,0:T(8,128)(2,1)} %fusion.69.q_ref, bf16[2048,384]{1,0:T(8,128)(2,1)} %bitcast.193, s32[1,192]{1,0:T(1,128)} %broadcast_in_dim_tile.6.pos_ref, s32[1,192]{1,0:T(1,128)} %broadcast_in_dim_tile.7.doc_ref), custom_call_target="tpu_custom_call" | custom-call | tf_op jit(solution)/shard_map/attend/pallas_call | solution.py:259
  175.3 1.7 multiply_reduce_fusion.4
  177.8 11.5 %comm2.4 = bf16[4,64,576]{2,1,0:T(8,128)(2,1)} custom-call(bf16[64,576]{1,0:T(8,128)(2,1)} %multiply_convert_fusion.6.refs_0_), custom_call_target="tpu_custom_call" | custom-call | tf_op jit(solution)/shard_map/comm2/pallas_call | solution.py:183
  189.3 1.3 fusion.15
  190.6 1.3 fusion.19
  192.0 2.2 multiply_convert_fusion.2
  196.2 1.9 copy.40
  198.1 11.4 %comm3.6 = bf16[4,64,576]{2,1,0:T(8,128)(2,1)} custom-call(bf16[4,64,576]{2,1,0:T(8,128)(2,1)} %bitcast.223), custom_call_target="tpu_custom_call" | custom-call | tf_op jit(solution)/shard_map/comm3/pallas_call | solution.py:183
  211.0 2.3 convolution_convert_fusion.13.do_ref
  213.2 10.8 %attend_back.2 = (f32[64,576]{1,0:T(8,128)}, bf16[2048,384]{1,0:T(8,128)(2,1)}) custom-call(bf16[64,576]{1,0:T(8,128)(2,1)} %fusion.69.q_ref, bf16[64,576]{1,0:T(8,128)(2,1)} %convolution_convert_fusion.13.do_ref, bf16[64,576]{1,0:T(8,128)(2,1)} %get-tuple-element.47.o_ref, bf16[2048,384]{1,0:T(8,128)(2,1)} %bitcast.194, ...), custom_call_target="tpu_custom_call" | custom-call | tf_op jit(solution)/shard_map/attend_back/pallas_call | solution.py:312
  225.1 1.1 fusion.77
  226.3 4.6 comm4.2
  231.0 2.2 fusion.1.refs_0_
  233.2 25.1 %comm5.2 = bf16[16,64,384]{2,1,0:T(8,128)(2,1)} custom-call(bf16[16,64,384]{2,1,0:T(8,128)(2,1)} %fusion.1.refs_0_), custom_call_target="tpu_custom_call" | custom-call | tf_op jit(solution)/shard_map/comm5/pallas_call | solution.py:183
  258.3 1.3 convert_reduce_fusion.1
  259.9 1.9 fusion.66
  263.2 11.5 %comm2.5 = bf16[4,64,576]{2,1,0:T(8,128)(2,1)} custom-call(bf16[64,576]{1,0:T(8,128)(2,1)} %fusion.65.refs_0_.refs_3_), custom_call_target="tpu_custom_call" | custom-call | tf_op jit(solution)/shard_map/comm2/pallas_call | solution.py:183
  274.7 1.7 multiply_convert_fusion
  278.5 10.3 %comm3.7 = bf16[4,64,576]{2,1,0:T(8,128)(2,1)} custom-call(bf16[4,64,576]{2,1,0:T(8,128)(2,1)} %bitcast.224), custom_call_target="tpu_custom_call" | custom-call | tf_op jit(solution)/shard_map/comm3/pallas_call | solution.py:183
  290.1 2.2 convolution_convert_fusion.12.do_ref
  292.3 10.6 %attend_back.3 = (f32[64,576]{1,0:T(8,128)}, bf16[2048,384]{1,0:T(8,128)(2,1)}) custom-call(bf16[64,576]{1,0:T(8,128)(2,1)} %fusion.71.q_ref, bf16[64,576]{1,0:T(8,128)(2,1)} %convolution_convert_fusion.12.do_ref, bf16[64,576]{1,0:T(8,128)(2,1)} %get-tuple-element.43.o_ref, bf16[2048,384]{1,0:T(8,128)(2,1)} %bitcast.192, ...), custom_call_target="tpu_custom_call" | custom-call | tf_op jit(solution)/shard_map/attend_back/pallas_call | solution.py:312
  304.1 1.1 fusion.79
  305.2 4.6 comm4.3
  309.9 2.2 fusion.refs_0_
  312.1 25.0 %comm5.3 = bf16[16,64,384]{2,1,0:T(8,128)(2,1)} custom-call(bf16[16,64,384]{2,1,0:T(8,128)(2,1)} %fusion.refs_0_), custom_call_target="tpu_custom_call" | custom-call | tf_op jit(solution)/shard_map/comm5/pallas_call | solution.py:183
  337.2 1.3 convert_reduce_fusion
  338.9 2.6 fusion.56
  343.1 1.6 pad_maximum_fusion.1.refs_5_
  344.7 1.1 convolution_convert_fusion.5.refs_10_
  345.8 1.1 convolution_convert_fusion.7.refs_8_
  347.0 1.1 convolution_convert_fusion.9.refs_6_
  349.1 1.6 pad_maximum_fusion.refs_4_
  353.0 1.7 select_bitcast_fusion
  354.7 2.2 convolution_convert_fusion.4.refs_11_
  356.9 2.2 convolution_convert_fusion.10
  359.2 1.9 copy.39
  361.0 10.4 %comm3.5 = bf16[4,64,576]{2,1,0:T(8,128)(2,1)} custom-call(bf16[4,64,576]{2,1,0:T(8,128)(2,1)} %bitcast.225), custom_call_target="tpu_custom_call" | custom-call | tf_op jit(solution)/shard_map/comm3/pallas_call | solution.py:183
  373.1 10.9 %comm6.1 = (bf16[64,576]{1,0:T(8,128)(2,1)}, bf16[64,576]{1,0:T(8,128)(2,1)}, bf16[576,1536]{1,0:T(8,128)(2,1)}, bf16[576,384]{1,0:T(8,128)(2,1)}, bf16[576,384]...) custom-call(bf16[64,576]{1,0:T(8,128)(2,1)} %copy-done.12, bf16[64,576]{1,0:T(8,128)(2,1)} %get-tuple-element.108.refs_1_, ...), custom_call_target="tpu_custom_call" | custom-call | tf_op jit(solution)/shard_map/comm6/pallas_call | solution.py:183
  384.0 1.4 select_add_fusion.refs_4_
  385.4 2.1 add_convert_fusion.1
  389.5 2.6 add_convert_fusion
  392.1 2.4 reshape.424
  394.5 1.4 copy.53
  395.9 49.2 %comm7.1 = (bf16[4,4,36,1536]{3,2,1,0:T(8,128)(2,1)}, bf16[4,144,384]{2,1,0:T(8,128)(2,1)}, bf16[4,144,384]{2,1,0:T(8,128)(2,1)}, bf16[4,96,576]{2,1,0:T(8,128)(2,1)}, f32[16,2,576]{2,1,0:T(2,128)}) custom-call(bf16[4,4,36,1536]{3,2,1,0:T(8,128)(2,1)} %bitcast.199, bf16[4,144,384]{2,1,0:T(8,128)(2,1)} %bitcast.219, bf16[4,144,384]{2,1,0:T(8,128)(2,1)} %bitcast.218, ...), custom_call_target="tpu_custom_call" | custom-call | tf_op jit(solution)/shard_map/comm7/pallas_call | solution.py:183
  445.1 2.8 reduce_sum.250.refs_0_
  448.0 14.3 %comm8.1 = bf16[4,36,1536]{2,1,0:T(8,128)(2,1)} custom-call(bf16[4,36,1536]{2,1,0:T(8,128)(2,1)} %reduce_sum.250.refs_0_), custom_call_target="tpu_custom_call" | custom-call | tf_op jit(solution)/shard_map/comm8/pallas_call | solution.py:183
  462.2 1.8 reduce_sum.251.refs_0_
  466.2 24.0 %comm9.1 = (bf16[4,36,1536]{2,1,0:T(8,128)(2,1)}, bf16[4,144,384]{2,1,0:T(8,128)(2,1)}, bf16[4,144,384]{2,1,0:T(8,128)(2,1)}, bf16[4,96,576]{2,1,0:T(8,128)(2,1)}) custom-call(bf16[36,1536]{1,0:T(8,128)(2,1)} %reduce_sum.251.refs_0_, bf16[144,384]{1,0:T(8,128)(2,1)} %reduce_sum.252.refs_1_, bf16[144,384]{1,0:T(8,128)(2,1)} %reduce_sum.253.refs_2_, ...), custom_call_target="tpu_custom_call" | custom-call | tf_op jit(solution)/shard_map/comm9/pallas_call | solution.py:183
  490.3 1.2 bitcast_convert_fusion
  491.4 1.2 copy.49
  (210 shorter events, 39.3 us)
Async XLA Ops:
  0.6 5.7 %copy-start.54 = (f32[1,576]{1,0:T(1,128)S(1)}, f32[1,576]{1,0:T(1,128)}, u32[]{:S(2)}) copy-start(f32[1,576]{1,0:T(1,128)} %param.14) | copy-start | bytes 6916
  0.7 5.7 %copy-start.53 = (f32[1,576]{1,0:T(1,128)S(1)}, f32[1,576]{1,0:T(1,128)}, u32[]{:S(2)}) copy-start(f32[1,576]{1,0:T(1,128)} %param.19) | copy-start | bytes 6916
  2.2 60.2 %copy-start.31 = (bf16[2,64,576]{2,1,0:T(8,128)(2,1)S(1)}, bf16[2,64,576]{2,1,0:T(8,128)(2,1)}, u32[]{:S(2)}) copy-start(bf16[2,64,576]{2,1,0:T(8,128)(2,1)} %param.12) | copy-start | bytes 442372
  93.5 25.1 %copy-start.11 = (bf16[2,576,384]{2,1,0:T(8,128)(2,1)S(1)}, bf16[2,576,384]{2,1,0:T(8,128)(2,1)}, u32[]{:S(2)}) copy-start(bf16[2,576,384]{2,1,0:T(8,128)(2,1)} %get-tuple-element.44) | copy-start | bytes 2654212
  104.2 15.8 %copy-start.16 = (bf16[2,576,384]{2,1,0:T(8,128)(2,1)S(1)}, bf16[2,576,384]{2,1,0:T(8,128)(2,1)}, u32[]{:S(2)}) copy-start(bf16[2,576,384]{2,1,0:T(8,128)(2,1)} %get-tuple-element.45) | copy-start | bytes 2654212
  118.6 3.6 copy-start.20
  120.0 2.2 copy-start.41
  122.2 16.6 %copy-start.29 = (bf16[256,384]{1,0:T(8,128)(2,1)}, bf16[256,384]{1,0:T(8,128)(2,1)S(1)}, u32[]{:S(2)}) copy-start(bf16[256,384]{1,0:T(8,128)(2,1)S(1)} %get-tuple-element.160) | copy-start | bytes 589828
  137.1 235.3 %copy-start.12 = (bf16[64,576]{1,0:T(8,128)(2,1)}, bf16[64,576]{1,0:T(8,128)(2,1)S(1)}, u32[]{:S(2)}) copy-start(bf16[64,576]{1,0:T(8,128)(2,1)S(1)} %get-tuple-element.110.refs_0_) | copy-start | bytes 221188
  175.3 16.7 %copy-start.48 = (bf16[4,64,576]{2,1,0:T(8,128)(2,1)S(1)}, bf16[4,64,576]{2,1,0:T(8,128)(2,1)}, u32[]{:S(2)}) copy-start(bf16[4,64,576]{2,1,0:T(8,128)(2,1)} %get-tuple-element.48) | copy-start | bytes 884740
  194.1 0.7 copy-start.21
  194.1 1.0 copy-start.23
  196.2 14.6 %copy-start.49 = (f32[2,64,576]{2,1,0:T(8,128)S(1)}, f32[2,64,576]{2,1,0:T(8,128)}, u32[]{:S(2)}) copy-start(f32[2,64,576]{2,1,0:T(8,128)} %param.23) | copy-start | bytes 884740
  211.0 51.5 %copy-start.13 = (f32[64,576]{1,0:T(8,128)}, f32[64,576]{1,0:T(8,128)S(1)}, u32[]{:S(2)}) copy-start(f32[64,576]{1,0:T(8,128)S(1)} %bitcast_add_fusion) | copy-start | bytes 442372
  225.1 5.9 %copy-start.10 = (bf16[2048,384]{1,0:T(8,128)(2,1)S(1)}, bf16[2048,384]{1,0:T(8,128)(2,1)}, u32[]{:S(2)}) copy-start(bf16[2048,384]{1,0:T(8,128)(2,1)} %get-tuple-element.51) | copy-start | bytes 4718596
  226.3 33.6 %copy-start.43 = (bf16[64,576]{1,0:T(8,128)(2,1)}, bf16[64,576]{1,0:T(8,128)(2,1)S(1)}, u32[]{:S(2)}) copy-start(bf16[64,576]{1,0:T(8,128)(2,1)S(1)} %fusion.77) | copy-start | bytes 221188
  259.6 15.1 %copy-start.42 = (f32[256,384]{1,0:T(8,128)S(1)}, f32[256,384]{1,0:T(8,128)}, u32[]{:S(2)}) copy-start(f32[256,384]{1,0:T(8,128)} %copy-done.41) | copy-start | bytes 1179652
  274.7 2.5 copy-start.17
  276.5 0.7 copy-start.25
  276.5 0.7 copy-start.27
  277.2 12.8 %copy-start.15 = (bf16[64,576]{1,0:T(8,128)(2,1)S(1)}, bf16[64,576]{1,0:T(8,128)(2,1)}, u32[]{:S(2)}) copy-start(bf16[64,576]{1,0:T(8,128)(2,1)} %fusion.65.refs_0_.refs_3_) | copy-start | bytes 221188
  304.0 5.9 %copy-start.9 = (bf16[2048,384]{1,0:T(8,128)(2,1)S(1)}, bf16[2048,384]{1,0:T(8,128)(2,1)}, u32[]{:S(2)}) copy-start(bf16[2048,384]{1,0:T(8,128)(2,1)} %get-tuple-element.54) | copy-start | bytes 4718596
  312.1 26.7 %copy-start.32 = (bf16[2,64,576]{2,1,0:T(8,128)(2,1)S(1)}, bf16[2,64,576]{2,1,0:T(8,128)(2,1)}, u32[]{:S(2)}) copy-start(bf16[2,64,576]{2,1,0:T(8,128)(2,1)} %param.12) | copy-start | bytes 442372
  337.2 4.9 copy-start.44
  338.8 3.9 copy-start.14
  338.8 3.9 copy-start.46
  343.0 1.7 copy-start.19
  343.0 1.6 copy-start.30
  343.1 2.8 copy-start.3
  343.1 2.8 copy-start.28
  344.7 2.3 copy-start.26
  345.8 2.8 copy-start.45
  349.1 1.7 copy-start.1
  349.1 1.7 copy-start
  349.1 1.7 copy-start.24
  349.1 2.8 copy-start.22
  373.1 12.3 %copy-start.4 = (bf16[384,576]{1,0:T(8,128)(2,1)S(1)}, bf16[384,576]{1,0:T(8,128)(2,1)}, u32[]{:S(2)}) copy-start(bf16[384,576]{1,0:T(8,128)(2,1)} %convolution_convert_fusion.5.refs_10_) | copy-start | bytes 1327108
  384.0 3.5 copy-start.6
  384.0 3.5 copy-start.8
  384.0 3.5 copy-start.38
  385.4 3.1 copy-start.5
  385.4 3.1 copy-start.7
  385.4 3.1 copy-start.37
  387.6 1.9 copy-start.2
  387.6 1.9 copy-start.18
  445.1 18.9 %copy-start.33 = (bf16[4,96,576]{2,1,0:T(8,128)(2,1)S(1)}, bf16[4,96,576]{2,1,0:T(8,128)(2,1)}, u32[]{:S(2)}) copy-start(bf16[4,96,576]{2,1,0:T(8,128)(2,1)} %get-tuple-element.66) | copy-start | bytes 1327108
  445.1 19.7 %copy-start.36 = (bf16[4,144,384]{2,1,0:T(8,128)(2,1)S(1)}, bf16[4,144,384]{2,1,0:T(8,128)(2,1)}, u32[]{:S(2)}) copy-start(bf16[4,144,384]{2,1,0:T(8,128)(2,1)} %get-tuple-element.64) | copy-start | bytes 1327108
  448.0 17.5 %copy-start.35 = (bf16[4,144,384]{2,1,0:T(8,128)(2,1)S(1)}, bf16[4,144,384]{2,1,0:T(8,128)(2,1)}, u32[]{:S(2)}) copy-start(bf16[4,144,384]{2,1,0:T(8,128)(2,1)} %get-tuple-element.65) | copy-start | bytes 1327108
  490.3 2.4 copy-start.34
  492.7 1.8 copy-start.40
  492.7 2.7 copy-start.39
  493.7 2.7 copy-start.52
  493.7 3.4 copy-start.47
  493.7 3.4 copy-start.51
  493.7 4.1 copy-start.50

commit v2 on v1

--- a/solution.py
+++ b/solution.py
@@ -52,27 +52,41 @@
     sems = refs[n_in + n_ops :]
     section = lax.axis_index("section")
     partner = {"section": 1 - section}
-    groups = []
-    swaps = False
-    for kind, axes in plan:
-        if kind in ("swap2", "agswap", "swap"):
+    n_wt, n_ctx = sizes["wt"], sizes["ctx"]
+    w, c = lax.axis_index("wt"), lax.axis_index("ctx")
+    left, right = {"wt": lax.rem(w + n_wt - 1, n_wt)}, {"wt": lax.rem(w + 1, n_wt)}
+    has_left, has_right = w > 0, w < n_wt - 1
+    groups, chain, swaps = [], False, False
+    for kind, axes, only in plan:
+        if kind in ("swap2", "swap", "to", "chainswap", "wide"):
             swaps = True
-        if kind in ("ag", "a2a", "agswap") and axes not in groups:
+        if kind in ("chain", "chainswap", "wide"):
+            chain = True
+        if kind == "wide" and ("ctx",) not in groups:
+            groups.append(("ctx",))
+        if kind in ("ag", "a2a") and axes not in groups:
             groups.append(axes)
+    if ("wt",) in groups:
+        chain = False
     barrier = pltpu.get_barrier_semaphore()
+
+    def greet(where):
+        pl.semaphore_signal(barrier, inc=1, device_id=where, device_id_type=MESH)
+
     expected = 0
     for axes in groups:
         n = group_of(axes, sizes)
         me = my_index(axes, sizes)
         for d in range(1, n):
-            peer = lax.rem(me + d, n)
-            pl.semaphore_signal(
-                barrier, inc=1, device_id=device_at(axes, peer, sizes), device_id_type=MESH
-            )
+            greet(device_at(axes, lax.rem(me + d, n), sizes))
             expected += 1
     if swaps:
-        pl.semaphore_signal(barrier, inc=1, device_id=partner, device_id_type=MESH)
+        greet(partner)
         expected += 1
+    if chain:
+        pl.when(has_left)(lambda: greet(left))
+        pl.when(has_right)(lambda: greet(right))
+        expected += lax.div(w + n_wt - 1, n_wt) + lax.div(2 * n_wt - 2 - w, n_wt)
     pl.semaphore_wait(barrier, expected)
 
     def remote(src, dst, send, recv, where):
@@ -81,102 +95,200 @@
             device_id_type=MESH,
         )
 
-    pending = []
-    forwards = []
-    at = 0
-    for slot, (kind, axes) in enumerate(plan):
-        out = outs[slot]
-        send, recv, local, fsend, frecv = sems[5 * slot : 5 * slot + 5]
-        if kind == "swap2":
-            first, second = ins[at], ins[at + 1]
-            at += 2
-
-            @pl.when(section == 0)
-            def _():
-                remote(second, out, send.at[0], recv.at[0], partner).start()
-
-            @pl.when(section == 1)
-            def _():
-                remote(first, out, send.at[0], recv.at[0], partner).start()
-
-            pending.append(remote(first, out, send.at[0], recv.at[0], partner))
-            continue
-        x = ins[at]
-        at += 1
-        if kind == "swap":
-            copy = remote(x.at[1 - section], out, send.at[0], recv.at[0], partner)
-            copy.start()
-            pending.append(copy)
-            continue
+    second_phase = []
+    last_phase = []
+
+    def run(only, f):
+        if only is None:
+            f()
+        else:
+            pl.when(section == only)(lambda: (f(), None)[1])
+
+    def simple(out, sem, slot_source):
+        send, recv = sem[0], sem[1]
+        copy = remote(slot_source, out, send.at[0], recv.at[0], partner)
+        copy.start()
+        return copy
+
+    def start_group(kind, axes, x, out, sem):
+        send, recv, local = sem[0], sem[1], sem[2]
         n = group_of(axes, sizes)
         me = my_index(axes, sizes)
-        target = out.at[section] if kind == "agswap" else out
         for d in range(1, n):
             peer = lax.rem(me + d, n)
             source = x.at[peer] if kind == "a2a" else x
             remote(
-                source, target.at[me], send.at[peer], recv.at[me], device_at(axes, peer, sizes)
+                source, out.at[me], send.at[peer], recv.at[me], device_at(axes, peer, sizes)
             ).start()
-        own = pltpu.make_async_copy(x.at[me] if kind == "a2a" else x, target.at[me], local)
-        own.start()
-        if kind == "agswap":
-            forward = remote(x, target.at[me], fsend.at[me], frecv.at[me], partner)
-            forward.start()
-        forwards.append((kind, axes, x, out, target, own, sems[5 * slot : 5 * slot + 5]))
-    for kind, axes, x, out, target, own, (send, recv, local, fsend, frecv) in forwards:
+        pltpu.make_async_copy(x.at[me] if kind == "a2a" else x, out.at[me], local).start()
+
+    def end_group(kind, axes, x, out, sem):
+        send, recv, local = sem[0], sem[1], sem[2]
         n = group_of(axes, sizes)
         me = my_index(axes, sizes)
         for d in range(1, n):
             peer = lax.rem(me + n - d, n)
             where = device_at(axes, peer, sizes)
             source = x.at[peer] if kind == "a2a" else x
-            copy = remote(source, target.at[peer], send.at[peer], recv.at[peer], where)
+            copy = remote(source, out.at[peer], send.at[peer], recv.at[peer], where)
             copy.wait_recv()
-            if kind == "agswap":
-                remote(
-                    target.at[peer], target.at[peer], fsend.at[peer], frecv.at[peer], partner
-                ).start()
-        own.wait()
-        for d in range(1, n):
-            peer = lax.rem(me + n - d, n)
-            where = device_at(axes, peer, sizes)
-            source = x.at[peer] if kind == "a2a" else x
-            remote(source, target.at[peer], send.at[peer], recv.at[peer], where).wait_send()
-        if kind == "agswap":
-            other = out.at[1 - section]
-            for d in range(n):
-                peer = lax.rem(me + n - d, n)
-                copy = remote(
-                    target.at[peer], other.at[peer], fsend.at[peer], frecv.at[peer], partner
-                )
+            copy.wait_send()
+        pltpu.make_async_copy(x.at[me] if kind == "a2a" else x, out.at[me], local).wait()
+
+    at = 0
+    for slot, (kind, axes, only) in enumerate(plan):
+        out = outs[slot]
+        sem = sems[6 * slot : 6 * slot + 6]
+        send, recv, local, fsend, frecv, lsend = sem
+        x = ins[at]
+        at += 1
+        if kind == "swap2":
+            second = ins[at]
+            at += 1
+            run(0, functools.partial(simple, out, sem, second))
+            run(1, functools.partial(simple, out, sem, x))
+
+            def end(x=x, out=out, sem=sem):
+                copy = remote(x, out, sem[0].at[0], sem[1].at[0], partner)
                 copy.wait_send()
                 copy.wait_recv()
-    for copy in pending:
-        copy.wait_send()
-        copy.wait_recv()
+
+            last_phase.append(end)
+        elif kind == "swap":
+            copy = simple(out, sem, x.at[1 - section])
+            last_phase.append(lambda copy=copy: (copy.wait_send(), copy.wait_recv()))
+        elif kind == "to":
+            run(1 - only, functools.partial(simple, out, sem, x))
+            copy = remote(x, out, send.at[0], recv.at[0], partner)
+            last_phase.append(lambda copy=copy, only=only: run(1 - only, copy.wait_send))
+            last_phase.append(lambda copy=copy, only=only: run(only, copy.wait_recv))
+        elif kind in ("ag", "a2a"):
+            run(only, functools.partial(start_group, kind, axes, x, out, sem))
+            last_phase.append(
+                functools.partial(
+                    run, only, functools.partial(end_group, kind, axes, x, out, sem)
+                )
+            )
+        else:
+            swap = kind != "chain"
+            wide = kind == "wide"
+            mine = out.at[section] if swap else out
+            column = mine.at[c] if wide else mine
+            base = c * n_wt if wide else 0
+
+            def spread(j, src, column=column, mine=mine, base=base, sem=sem, swap=swap, wide=wide):
+                send, recv, local, fsend, frecv, lsend = sem
+                if wide:
+                    for d in range(1, n_ctx):
+                        peer = lax.rem(c + d, n_ctx)
+                        remote(
+                            src, column.at[j], send.at[n_wt + peer * n_wt + j],
+                            recv.at[base + j], {"ctx": peer},
+                        ).start()
+                if swap:
+                    remote(src, column.at[j], fsend.at[base + j], frecv.at[base + j], partner).start()
+
+            def hop(j, src, where, which, column=column, base=base, sem=sem):
+                return remote(src, column.at[j], which, sem[1].at[base + j], where)
+
+            pl.when(has_right)(lambda h=hop, x=x, send=send: h(w, x, right, send.at[w]).start())
+            pl.when(has_left)(lambda h=hop, x=x, lsend=lsend: h(w, x, left, lsend).start())
+            spread(w, x)
+            pltpu.make_async_copy(x, column.at[w], local).start()
+            second_phase.append((x, out, mine, column, base, sem, swap, wide, spread, hop))
+
+    for t in range(1, n_wt):
+        for x, out, mine, column, base, sem, swap, wide, spread, hop in second_phase:
+            send, recv, local, fsend, frecv, lsend = sem
+
+            @pl.when(w >= t)
+            def _():
+                j = w - t
+                hop(j, x, left, send.at[j]).wait_recv()
+                pl.when(has_right)(lambda: hop(j, column.at[j], right, send.at[j]).start())
+                spread(j, column.at[j])
+
+            @pl.when(w + t < n_wt)
+            def _():
+                j = w + t
+                hop(j, x, right, send.at[j]).wait_recv()
+                pl.when(has_left)(lambda: hop(j, column.at[j], left, send.at[j]).start())
+                spread(j, column.at[j])
+
+    for x, out, mine, column, base, sem, swap, wide, spread, hop in second_phase:
+        send, recv, local, fsend, frecv, lsend = sem
+        if wide:
+            for d in range(1, n_ctx):
+                peer = lax.rem(c + n_ctx - d, n_ctx)
+                for j in range(n_wt):
+                    k = peer * n_wt + j
+                    got = mine.at[peer].at[j]
+                    remote(x, got, send.at[n_wt + k], recv.at[k], {"ctx": peer}).wait_recv()
+                    remote(got, got, fsend.at[k], frecv.at[k], partner).start()
+
+    for end in last_phase:
+        end()
+
+    for x, out, mine, column, base, sem, swap, wide, spread, hop in second_phase:
+        send, recv, local, fsend, frecv, lsend = sem
+        pl.when(has_right)(lambda: hop(w, x, right, send.at[w]).wait_send())
+        pl.when(has_left)(lambda: hop(w, x, left, lsend).wait_send())
+        for t in range(1, n_wt):
+            pl.when((w >= t) & has_right)(
+                lambda: hop(w - t, x, right, send.at[w - t]).wait_send()
+            )
+            pl.when((w + t < n_wt) & has_left)(
+                lambda: hop(w + t, x, left, send.at[w + t]).wait_send()
+            )
+        pltpu.make_async_copy(x, column.at[w], local).wait()
+        if wide:
+            for d in range(1, n_ctx):
+                peer = lax.rem(c + d, n_ctx)
+                for j in range(n_wt):
+                    remote(
+                        x, column.at[j], send.at[n_wt + peer * n_wt + j], recv.at[j],
+                        {"ctx": peer},
+                    ).wait_send()
+        if swap:
+            count = n_ctx * n_wt if wide else n_wt
+            for k in range(count):
+                here = mine.at[k // n_wt].at[k % n_wt] if wide else mine.at[k]
+                copy = remote(here, here, fsend.at[k], frecv.at[k], partner)
+                copy.wait_send()
+                copy.wait_recv()
 
 
 def communicate(sizes, *ops):
     plan, arrays, shapes, scratch = [], [], [], []
-    for kind, axes, x in ops:
-        plan.append((kind, axes))
+    n_wt, n_ctx = sizes["wt"], sizes["ctx"]
+    for kind, axes, x, *only in ops:
+        plan.append((kind, axes, only[0] if only else None))
+        n = 1
         if kind == "swap2":
             arrays.extend(x)
-            n, shape, dtype = 1, x[0].shape, x[0].dtype
+            shape, dtype = x[0].shape, x[0].dtype
         else:
             arrays.append(x)
-            n, shape, dtype = 1, x.shape, x.dtype
+            shape, dtype = x.shape, x.dtype
             if kind == "swap":
                 shape = x.shape[1:]
-            else:
+            elif kind == "a2a":
                 n = group_of(axes, sizes)
-                if kind == "ag":
-                    shape = (n,) + x.shape
-                elif kind == "agswap":
-                    shape = (2, n) + x.shape
+            elif kind == "ag":
+                n = group_of(axes, sizes)
+                shape = (n,) + x.shape
+            elif kind == "chain":
+                n = n_wt
+                shape = (n_wt,) + x.shape
+            elif kind == "chainswap":
+                n = n_wt
+                shape = (2, n_wt) + x.shape
+            elif kind == "wide":
+                n = n_wt * (n_ctx + 1)
+                shape = (2, n_ctx, n_wt) + x.shape
         shapes.append(jax.ShapeDtypeStruct(shape, dtype))
         dma = pltpu.SemaphoreType.DMA
-        scratch += [dma((n,)), dma((n,)), dma(()), dma((n,)), dma((n,))]
+        scratch += [dma((n,)), dma((n,)), dma(()), dma((n,)), dma((n,)), dma(())]
     key = (tuple(plan), tuple((a.shape, str(a.dtype)) for a in arrays))
     ident = IDS.setdefault(key, len(IDS))
     space = pl.BlockSpec(memory_space=pltpu.VMEM)
@@ -355,12 +467,12 @@
     gains = jnp.concatenate([attn_gain, mlp_gain], 0)
     weights, gates, ups, downs, all_gains, cot_rows = communicate(
         sizes,
-        ("agswap", ("wt",), fused),
+        ("chainswap", (), fused),
         ("ag", ("section",), w_gate[0]),
         ("ag", ("section",), w_up[0]),
         ("ag", ("section",), w_down[0]),
         ("ag", ("section",), gains),
-        ("ag", ("wt",), cot.astype(BF)),
+        ("chain", (), cot.astype(BF)),
     )
     weights = weights.reshape(2, width, fused.shape[1])
     w_qkv = weights[:, :, : qw + 2 * KVW]
@@ -389,7 +501,7 @@
         k = rope(qkv[:, qw : qw + KVW], cos, sin).astype(BF)
         v = qkv[:, qw + KVW :].astype(BF)
         (kv,) = communicate(
-            sizes, ("agswap", ("ctx", "wt"), jnp.concatenate([k, v], 1))
+            sizes, ("wide", (), jnp.concatenate([k, v], 1))
         )
         kv = kv.reshape(keys, 2 * KVW)
         o, lse = attend(q, kv, pos_row, doc_row)
@@ -397,28 +509,57 @@
         r2 = lax.rsqrt(jnp.mean(h2 * h2, -1, keepdims=True) + EPS)
         n2 = h2 * r2
         z = (n2 * gm).astype(BF)
-        (zr,) = communicate(sizes, ("ag", ("wt",), z))
+        (zr,) = communicate(sizes, ("chain", (), z))
         zr = zr.reshape(n_wt * rows, width)
         g = nn(zr, gates[layer])
         up = nn(zr, ups[layer])
         act = (g * jax.nn.sigmoid(g) * up).astype(BF)
         branch = nn(act, downs[layer]).astype(BF).reshape(n_wt, rows, width)
-        (parts,) = communicate(sizes, ("a2a", ("wt",), branch))
-        out = (h2 + jnp.sum(parts.astype(F32), 0)).astype(BF)
         saved.append((n1, r1, u, q, kv, o, lse, n2, r2, zr, g, up, act))
-        h_in = out
         if layer == 0:
-            first_out = out
-    second_out = h_in
-
-    grads = [None, None]
+            (parts,) = communicate(sizes, ("a2a", ("wt",), branch))
+            h_in = first_out = (h2 + jnp.sum(parts.astype(F32), 0)).astype(BF)
+
+    def total(x):
+        return jnp.sum(x.astype(F32), 0)
+
+    def summed(own, other):
+        return (own.astype(F32) + other.astype(F32)).astype(BF)
+
+    hidden = w_gate.shape[2]
+    cols = fused.shape[1]
+    ctx = ("ctx",)
+    split = width // n_wt // n_ctx
+
+    def mlp_chunks(parts):
+        gate, lift, down = parts
+        return (
+            gate.reshape(n_ctx, width // n_ctx, hidden),
+            lift.reshape(n_ctx, width // n_ctx, hidden),
+            down.reshape(n_ctx, hidden // n_ctx, width),
+        )
+
+    def attn_chunks(x):
+        return x.reshape(n_wt, n_ctx, split, cols).transpose(1, 0, 2, 3)
+
+    def many(kind, axes, items, only):
+        return [(kind, axes, item, only) for item in items]
+
     e = cot
     er = cot_rows.reshape(n_wt * rows, width)
     for layer in (1, 0):
         ga, gm = all_gains[layer, 0], all_gains[layer, 1]
         n1, r1, u, q, kv, o, lse, n2, r2, zr, g, up, act = saved[layer]
         if layer == 0:
-            (er,) = communicate(sizes, ("ag", ("wt",), e))
+            er, attn1_theirs, gain1_theirs, *mlp1 = communicate(
+                sizes,
+                ("chain", (), e),
+                ("to", (), attn1, 1),
+                ("to", (), gain1, 1),
+                *many("a2a", ctx, mlp_chunks(mlp1), 1),
+            )
+            mlp1 = [total(item).astype(BF) for item in mlp1]
+            attn1 = attn_chunks(summed(attn1, attn1_theirs))
             er = er.reshape(n_wt * rows, width)
             e = e.astype(F32)
         g_down = tn(act, er)
@@ -428,9 +569,16 @@
         du = (da * g * s).astype(BF)
         g_gate = tn(zr, dg)
         g_up = tn(zr, du)
+        mlp = (g_gate.astype(BF), g_up.astype(BF), g_down.astype(BF))
         term = (nt(dg, gates[layer]) + nt(du, ups[layer])).astype(BF).reshape(n_wt, rows, width)
-        (parts,) = communicate(sizes, ("a2a", ("wt",), term))
-        dz = jnp.sum(parts.astype(F32), 0)
+        if layer == 1:
+            (parts,) = communicate(sizes, ("a2a", ("wt",), term))
+        else:
+            parts, attn1 = communicate(
+                sizes, ("a2a", ("wt",), term), ("a2a", ctx, attn1, 1)
+            )
+            attn1 = total(attn1).astype(BF)
+        dz = total(parts)
         g_gm = jnp.sum(dz * n2, 0)
         m2 = dz * gm
         dh2 = e + r2 * (m2 - n2 * jnp.mean(m2 * n2, -1, keepdims=True))
@@ -439,11 +587,30 @@
         do = nt(ob, w_out[layer]).astype(BF)
         dq, dkv = attend_back(q, do, o, kv, lse, pos_row, doc_row)
         dkv = dkv.reshape(micro, n_place, rows, 2 * KVW)
-        (theirs,) = communicate(sizes, ("swap", (), dkv))
+        if layer == 1:
+            theirs, *mlp1 = communicate(sizes, ("swap", (), dkv), *many("to", (), mlp, 1))
+            mlp1 = [summed(own, other) for own, other in zip(mlp, mlp1)]
+        else:
+            theirs, parts, *rest = communicate(
+                sizes,
+                ("swap", (), dkv),
+                ("a2a", ("wt",), branch),
+                *many("to", (), mlp, 0),
+                *many("ag", ctx, mlp1, 1),
+            )
+            mlp0 = mlp_chunks([summed(own, other) for own, other in zip(mlp, rest[:3])])
+            mlp1 = rest[3:]
+            second_out = (h2 + total(parts)).astype(BF)
         mine = lax.dynamic_index_in_dim(dkv, section, 0, keepdims=False)
-        both = (mine.astype(F32) + theirs.astype(F32)).astype(BF)
-        (pieces,) = communicate(sizes, ("a2a", ("ctx", "wt"), both))
-        dkv_own = jnp.sum(pieces.astype(F32), 0)
+        both = summed(mine, theirs)
+        if layer == 1:
+            (pieces,) = communicate(sizes, ("a2a", ("ctx", "wt"), both))
+        else:
+            pieces, attn1 = communicate(
+                sizes, ("a2a", ("ctx", "wt"), both), ("a2a", ("wt",), attn1, 1)
+            )
+            attn1 = total(attn1).astype(BF)
+        dkv_own = total(pieces)
         dqr = rope_back(dq, cos, sin).astype(BF)
         dkr = rope_back(dkv_own[:, :KVW], cos, sin).astype(BF)
         dvr = dkv_own[:, KVW:].astype(BF)
@@ -453,65 +620,44 @@
         g_ga = jnp.sum(du_in * n1, 0)
         m1 = du_in * ga
         e = (dh2 + r1 * (m1 - n1 * jnp.mean(m1 * n1, -1, keepdims=True))).astype(BF)
-        grads[layer] = (
-            jnp.concatenate([g_qkv, g_o], 1).astype(BF),
-            g_gate.astype(BF),
-            g_up.astype(BF),
-            g_down.astype(BF),
-            jnp.stack([g_ga, g_gm]),
-        )
+        attn = jnp.concatenate([g_qkv, g_o], 1).astype(BF)
+        gain = jnp.stack([g_ga, g_gm])
         if layer == 1:
-            second_grad = e
+            second_grad, attn1, gain1 = e, attn, gain
     first_grad = e
 
-    received = communicate(
+    other_out, other_grad, attn0, gain0, attn1, *mlp0 = communicate(
         sizes,
         ("swap2", (), (first_out, second_out)),
         ("swap2", (), (first_grad, second_grad)),
-        *[("swap2", (), pair) for pair in zip(grads[0], grads[1])],
+        ("to", (), attn, 0),
+        ("to", (), gain, 0),
+        ("ag", ctx, attn1, 1),
+        *many("a2a", ctx, mlp0, 0),
     )
-
-    def keep(pair):
-        return jnp.where(section == 0, pair[0], pair[1])
-
-    def whole(own, other):
-        return jnp.where(section == 0, jnp.stack([own, other]), jnp.stack([other, own]))
-
-    acts = whole(keep((first_out, second_out)), received[0])
-    dacts = whole(keep((first_grad, second_grad)), received[1])
-    summed = [
-        keep(pair).astype(F32) + other.astype(F32)
-        for pair, other in zip(zip(grads[0], grads[1]), received[2:])
-    ]
-    g_attn, g_gate, g_up, g_down, g_gain = summed
-    cols = g_attn.shape[1]
-    split = width // n_wt // n_ctx
-    g_attn = (
-        g_attn.astype(BF).reshape(n_wt, n_ctx, split, cols).transpose(1, 0, 2, 3)
+    mlp0 = [total(item).astype(BF) for item in mlp0]
+    gain = jnp.where(section == 0, gain + gain0, gain1 + gain1_theirs)
+    attn0, gain = communicate(
+        sizes,
+        ("a2a", ctx, attn_chunks(summed(attn, attn0)), 0),
+        ("ag", ("ctx", "wt"), gain),
     )
-    hidden = g_gate.shape[1]
-    r_attn, r_gate, r_up, r_down, r_gain = communicate(
-        sizes,
-        ("a2a", ("ctx",), g_attn),
-        ("a2a", ("ctx",), g_gate.astype(BF).reshape(n_ctx, width // n_ctx, hidden)),
-        ("a2a", ("ctx",), g_up.astype(BF).reshape(n_ctx, width // n_ctx, hidden)),
-        ("a2a", ("ctx",), g_down.astype(BF).reshape(n_ctx, hidden // n_ctx, width)),
-        ("ag", ("ctx", "wt"), g_gain),
+    attn0, *mlp0 = communicate(
+        sizes, ("a2a", ("wt",), total(attn0).astype(BF), 0), *many("ag", ctx, mlp0, 0)
     )
-
-    def total(x):
-        return jnp.sum(x.astype(F32), 0)
-
-    (p_attn,) = communicate(sizes, ("a2a", ("wt",), total(r_attn).astype(BF)))
-    f_attn, f_gate, f_up, f_down = communicate(
-        sizes,
-        ("ag", ("ctx",), total(p_attn).astype(BF)),
-        ("ag", ("ctx",), total(r_gate).astype(BF)),
-        ("ag", ("ctx",), total(r_up).astype(BF)),
-        ("ag", ("ctx",), total(r_down).astype(BF)),
-    )
-    f_attn = f_attn.reshape(width // n_wt, cols).astype(F32)
-    gain = lax.dynamic_slice_in_dim(total(r_gain), wt * (width // n_wt), width // n_wt, 1)
+    (attn0,) = communicate(sizes, ("ag", ctx, total(attn0).astype(BF), 0))
+
+    def keep(first, second):
+        return jnp.where(section == 0, first, second)
+
+    def whole(first, second, other):
+        return jnp.where(section == 0, jnp.stack([first, other]), jnp.stack([other, second]))
+
+    acts = whole(first_out, second_out, other_out)
+    dacts = whole(first_grad, second_grad, other_grad)
+    f_attn = keep(attn0, attn1).reshape(width // n_wt, cols).astype(F32)
+    f_gate, f_up, f_down = [keep(a, b).astype(F32) for a, b in zip(mlp0, mlp1)]
+    gain = lax.dynamic_slice_in_dim(total(gain), wt * (width // n_wt), width // n_wt, 1)
     return (
         acts[None],
         dacts[None],
@@ -521,9 +667,9 @@
         f_attn[None, :, qw + KVW : qw + 2 * KVW],
         f_attn[None, :, qw + 2 * KVW :],
         gain[1][None],
-        f_gate.reshape(1, width, hidden).astype(F32),
-        f_up.reshape(1, width, hidden).astype(F32),
-        f_down.reshape(1, hidden, width).astype(F32),
+        f_gate.reshape(1, width, hidden),
+        f_up.reshape(1, width, hidden),
+        f_down.reshape(1, hidden, width),
     )
 
 

time: 501 us -> 468 us (0.934)
  Pallas kernels: 383 us -> 339 us
  other arithmetic: 49.6 us -> 63.4 us
    pallas_call x18 -> x17, Pallas kernels: 343 us -> 299 us  [communicate(): pl.pallas_call(functools.partial(comm_kernel, tuple(plan), sizes, len(arr...]
    reduce_sum x6 -> x16, other arithmetic: 6.85 us -> 20.1 us  [total(): return jnp.sum(x.astype(F32), 0)]
    convert_element_type x9 -> x12, other arithmetic: 14.2 us -> 21.6 us  [the longest x10 19.8 us: summed(): return (own.astype(F32) + other.astype(F32)).astype(BF)]
    reduce_sum x6 -> x1, other arithmetic: 6.68 us -> 1.04 us  [local(): h_in = first_out = (h2 + jnp.sum(parts.astype(F32), 0)).astype(BF)]
where the time goes in v2:
time: 468 us; the launch traced here: 466 us
  Pallas kernels  339 us (72%)
  other arithmetic  63.4 us (14%)
  matrix products  36.1 us (8%)
  local copies, waits for them, and re-layouts  25.4 us (5%)
    pallas_call x17, Pallas kernels, communicate(): pl.pallas_call(functools.partial(comm_kernel, tuple(plan), sizes, len(arr...  299 us
    pallas_call x2, Pallas kernels, attend_back(): pl.pallas_call(functools.partial(attend_back_kernel, 512 if keys % 512 ==...  21.3 us
    reduce_sum x16, other arithmetic, total(): return jnp.sum(x.astype(F32), 0)  20.1 us
    convert_element_type x10, other arithmetic, summed(): return (own.astype(F32) + other.astype(F32)).astype(BF)  19.8 us
    pallas_call x2, Pallas kernels, attend(): pl.pallas_call(functools.partial(attend_kernel, 512 if keys % 512 == 0 el...  18.8 us
    dot_general x10, matrix products, nn(): return jnp.dot(a, b, preferred_element_type=F32)  14.8 us
    dot_general x10, matrix products, nt(): lax.dot_general(a, b, (((1,), (1,)), ((), ())), preferred_element_type=F32)  11.7 us
    dot_general x10, matrix products, tn(): lax.dot_general(a, b, (((0,), (0,)), ((), ())), preferred_element_type=F32)  9.61 us

profile of v2, /device:TPU:0, one launch (start us, length us, event | category | flops | bytes accessed | tf_op | source)
XLA Modules:
  0.0 466.1 jit_solution(583750823008217616)
XLA Ops:
  1.8 2.1 concatenate.106.refs_0_
  5.5 1.6 bitcast_convert_fusion.3.refs_5_
  7.1 44.1 %comm0.1 = (bf16[2,4,144,1536]{3,2,1,0:T(8,128)(2,1)}, bf16[2,576,384]{2,1,0:T(8,128)(2,1)}, bf16[2,576,384]{2,1,0:T(8,128)(2,1)}, bf16[2,384,576]{2,1,0:T(8,128...) custom-call(bf16[144,1536]{1,0:T(8,128)(2,1)} %concatenate.106.refs_0_, bf16[576,384]{1,0:T(8,128)(2,1)} %bitcast.244, ...), custom_call_target="tpu_custom_call" | custom-call | tf_op jit(solution)/shard_map/comm0/pallas_call | solution.py:295
  52.2 1.7 fusion.5
  56.0 19.2 %comm1.2 = bf16[2,4,4,64,384]{4,3,2,1,0:T(8,128)(2,1)} custom-call(bf16[64,384]{1,0:T(8,128)(2,1)} %pad_maximum_fusion.4.refs_0_), custom_call_target="tpu_custom_call" | custom-call | tf_op jit(solution)/shard_map/comm1/pallas_call | solution.py:295
  76.5 9.4 %attend.2 = (bf16[64,576]{1,0:T(8,128)(2,1)}, f32[3,192]{1,0:T(4,128)}) custom-call(bf16[64,576]{1,0:T(8,128)(2,1)} %fusion.71.q_ref, bf16[2048,384]{1,0:T(8,128)(2,1)} %bitcast.196, s32[1,192]{1,0:T(1,128)} %broadcast_in_dim_tile.6.pos_ref, s32[1,192]{1,0:T(1,128)} %broadcast_in_dim_tile.7.doc_ref), custom_call_target="tpu_custom_call" | custom-call | tf_op jit(solution)/shard_map/attend/pallas_call | solution.py:371
  86.0 1.8 multiply_reduce_fusion.5
  88.5 13.3 %comm2.2 = bf16[4,64,576]{2,1,0:T(8,128)(2,1)} custom-call(bf16[64,576]{1,0:T(8,128)(2,1)} %multiply_convert_fusion.7.refs_0_), custom_call_target="tpu_custom_call" | custom-call | tf_op jit(solution)/shard_map/comm2/pallas_call | solution.py:295
  101.8 1.4 fusion.26
  103.3 2.2 multiply_convert_fusion.5
  107.4 9.3 %comm3.2 = bf16[4,64,576]{2,1,0:T(8,128)(2,1)} custom-call(bf16[4,64,576]{2,1,0:T(8,128)(2,1)} %bitcast.236), custom_call_target="tpu_custom_call" | custom-call | tf_op jit(solution)/shard_map/comm3/pallas_call | solution.py:295
  117.9 1.7 fusion.7
  121.5 19.2 %comm1.3 = bf16[2,4,4,64,384]{4,3,2,1,0:T(8,128)(2,1)} custom-call(bf16[64,384]{1,0:T(8,128)(2,1)} %pad_maximum_fusion.5.refs_0_), custom_call_target="tpu_custom_call" | custom-call | tf_op jit(solution)/shard_map/comm1/pallas_call | solution.py:295
  140.8 9.4 %attend.3 = (bf16[64,576]{1,0:T(8,128)(2,1)}, f32[3,192]{1,0:T(4,128)}) custom-call(bf16[64,576]{1,0:T(8,128)(2,1)} %fusion.69.q_ref, bf16[2048,384]{1,0:T(8,128)(2,1)} %bitcast.198, s32[1,192]{1,0:T(1,128)} %broadcast_in_dim_tile.6.pos_ref, s32[1,192]{1,0:T(1,128)} %broadcast_in_dim_tile.7.doc_ref), custom_call_target="tpu_custom_call" | custom-call | tf_op jit(solution)/shard_map/attend/pallas_call | solution.py:371
  150.2 1.7 multiply_reduce_fusion.4
  152.7 13.4 %comm2.3 = bf16[4,64,576]{2,1,0:T(8,128)(2,1)} custom-call(bf16[64,576]{1,0:T(8,128)(2,1)} %multiply_convert_fusion.6.refs_0_), custom_call_target="tpu_custom_call" | custom-call | tf_op jit(solution)/shard_map/comm2/pallas_call | solution.py:295
  166.0 1.4 fusion.16
  167.8 2.2 multiply_convert_fusion.2
  172.0 9.3 %comm3.3 = bf16[4,64,576]{2,1,0:T(8,128)(2,1)} custom-call(bf16[4,64,576]{2,1,0:T(8,128)(2,1)} %bitcast.237), custom_call_target="tpu_custom_call" | custom-call | tf_op jit(solution)/shard_map/comm3/pallas_call | solution.py:295
  183.7 2.2 convolution_convert_fusion.13.do_ref
  185.9 10.6 %attend_back.2 = (f32[64,576]{1,0:T(8,128)}, bf16[2048,384]{1,0:T(8,128)(2,1)}) custom-call(bf16[64,576]{1,0:T(8,128)(2,1)} %fusion.69.q_ref, bf16[64,576]{1,0:T(8,128)(2,1)} %convolution_convert_fusion.13.do_ref, bf16[64,576]{1,0:T(8,128)(2,1)} %get-tuple-element.67.o_ref, bf16[2048,384]{1,0:T(8,128)(2,1)} %bitcast.199, ...), custom_call_target="tpu_custom_call" | custom-call | tf_op jit(solution)/shard_map/attend_back/pallas_call | solution.py:424
  197.6 1.1 convolution_convert_fusion.8.refs_2_
  198.8 1.1 convolution_convert_fusion.5.refs_3_
  199.9 7.2 %comm4.1 = (bf16[16,64,384]{2,1,0:T(8,128)(2,1)}, bf16[576,384]{1,0:T(8,128)(2,1)}, bf16[576,384]{1,0:T(8,128)(2,1)}, bf16[384,576]{1,0:T(8,128)(2,1)}) custom-call(bf16[2,16,64,384]{3,2,1,0:T(8,128)(2,1)} %bitcast.220, bf16[576,384]{1,0:T(8,128)(2,1)} %convolution_convert_fusion.9.refs_1_, bf16[576,384]{1,0:T(8,128)(2,1)} %convolution_convert_fusion.8.refs_2_, ...), custom_call_target="tpu_custom_call" | custom-call | tf_op jit(solution)/shard_map/comm4/pallas_call | solution.py:295
  207.1 2.2 fusion.1.refs_0_
  209.4 24.0 %comm5.1 = bf16[16,64,384]{2,1,0:T(8,128)(2,1)} custom-call(bf16[16,64,384]{2,1,0:T(8,128)(2,1)} %fusion.1.refs_0_), custom_call_target="tpu_custom_call" | custom-call | tf_op jit(solution)/shard_map/comm5/pallas_call | solution.py:295
  233.4 1.3 convert_reduce_fusion.1
  235.4 1.9 fusion.66
  239.0 1.6 pad_maximum_fusion.refs_1_
  243.9 18.1 %comm6.1 = (bf16[4,64,576]{2,1,0:T(8,128)(2,1)}, bf16[576,1536]{1,0:T(8,128)(2,1)}, f32[2,576]{1,0:T(2,128)}, bf16[4,144,384]{2,1,0:T(8,128)(2,1)}, bf16[4,144,3...) custom-call(bf16[64,576]{1,0:T(8,128)(2,1)} %fusion.65.refs_0_.refs_3_, bf16[576,1536]{1,0:T(8,128)(2,1)} %pad_maximum_fusion.refs_1_, ...), custom_call_target="tpu_custom_call" | custom-call | tf_op jit(solution)/shard_map/comm6/pallas_call | solution.py:295
  262.0 1.7 multiply_convert_fusion
  265.7 3.4 add_convert_fusion.1
  269.1 2.4 reshape.410
  271.5 1.5 copy.56
  273.0 10.8 %comm7.1 = (bf16[4,64,576]{2,1,0:T(8,128)(2,1)}, bf16[4,4,36,1536]{3,2,1,0:T(8,128)(2,1)}) custom-call(bf16[4,64,576]{2,1,0:T(8,128)(2,1)} %bitcast.235, bf16[4,4,36,1536]{3,2,1,0:T(8,128)(2,1)} %bitcast.201), custom_call_target="tpu_custom_call" | custom-call | tf_op jit(solution)/shard_map/comm7/pallas_call | solution.py:295
  285.2 2.3 convolution_convert_fusion.12.do_ref
  287.4 10.7 %attend_back.3 = (f32[64,576]{1,0:T(8,128)}, bf16[2048,384]{1,0:T(8,128)(2,1)}) custom-call(bf16[64,576]{1,0:T(8,128)(2,1)} %fusion.71.q_ref, bf16[64,576]{1,0:T(8,128)(2,1)} %convolution_convert_fusion.12.do_ref, bf16[64,576]{1,0:T(8,128)(2,1)} %get-tuple-element.63.o_ref, bf16[2048,384]{1,0:T(8,128)(2,1)} %bitcast.197, ...), custom_call_target="tpu_custom_call" | custom-call | tf_op jit(solution)/shard_map/attend_back/pallas_call | solution.py:424
  299.4 1.1 convolution_convert_fusion.7.refs_2_
  300.5 1.1 convolution_convert_fusion.6.refs_3_
  301.7 2.1 convolution_convert_fusion.4.refs_4_
  306.0 16.6 %comm8.1 = (bf16[16,64,384]{2,1,0:T(8,128)(2,1)}, bf16[4,64,576]{2,1,0:T(8,128)(2,1)}, bf16[576,384]{1,0:T(8,128)(2,1)}, bf16[576,384]{1,0:T(8,128)(2,1)}, bf16[...) custom-call(bf16[2,16,64,384]{3,2,1,0:T(8,128)(2,1)} %bitcast.218, ...), custom_call_target="tpu_custom_call" | custom-call | tf_op jit(solution)/shard_map/comm8/pallas_call | solution.py:295
  324.3 2.2 fusion.refs_0_
  326.6 2.8 reduce_sum.308.refs_1_
  329.3 28.4 %comm9.1 = (bf16[16,64,384]{2,1,0:T(8,128)(2,1)}, bf16[4,36,1536]{2,1,0:T(8,128)(2,1)}) custom-call(bf16[16,64,384]{2,1,0:T(8,128)(2,1)} %fusion.refs_0_, bf16[4,36,1536]{2,1,0:T(8,128)(2,1)} %reduce_sum.308.refs_1_), custom_call_target="tpu_custom_call" | custom-call | tf_op jit(solution)/shard_map/comm9/pallas_call | solution.py:295
  357.8 1.3 convert_reduce_fusion
  359.9 1.9 fusion.56
  363.5 1.6 pad_maximum_fusion.1.refs_4_
  365.8 1.8 reduce_sum.313.refs_6_
  367.6 2.0 add_convert_fusion.5
  369.6 1.9 add_convert_fusion.4
  371.5 1.9 add_convert_fusion.2
  373.4 20.0 %comm10.1 = (bf16[64,576]{1,0:T(8,128)(2,1)}, bf16[64,576]{1,0:T(8,128)(2,1)}, bf16[576,1536]{1,0:T(8,128)(2,1)}, f32[2,576]{1,0:T(2,128)}, bf16[4,36,1536]{2,1,...) custom-call(bf16[64,576]{1,0:T(8,128)(2,1)} %copy-done.10, ...), custom_call_target="tpu_custom_call" | custom-call | tf_op jit(solution)/shard_map/comm10/pallas_call | solution.py:295
  393.5 1.7 maximum_select_fusion.2
  395.1 1.7 maximum_select_fusion.3
  396.8 3.4 add_convert_fusion
  400.2 2.4 reshape.416
  402.6 1.5 copy.55
  404.7 22.4 %comm11.1 = (bf16[4,4,36,1536]{3,2,1,0:T(8,128)(2,1)}, f32[16,2,576]{2,1,0:T(2,128)}) custom-call(bf16[4,4,36,1536]{3,2,1,0:T(8,128)(2,1)} %bitcast.200, f32[2,576]{1,0:T(2,128)} %add_select_fusion.1.refs_1_), custom_call_target="tpu_custom_call" | custom-call | tf_op jit(solution)/shard_map/comm11/pallas_call | solution.py:295
  428.8 2.8 reduce_sum.315.refs_0_
  433.8 15.0 %comm12.1 = (bf16[4,36,1536]{2,1,0:T(8,128)(2,1)}, bf16[4,144,384]{2,1,0:T(8,128)(2,1)}, bf16[4,144,384]{2,1,0:T(8,128)(2,1)}, bf16[4,96,576]{2,1,0:T(8,128)(2,1)}) custom-call(bf16[4,36,1536]{2,1,0:T(8,128)(2,1)} %reduce_sum.315.refs_0_, bf16[144,384]{1,0:T(8,128)(2,1)} %reduce_sum.316.refs_1_, bf16[144,384]{1,0:T(8,128)(2,1)} %reduce_sum.317.refs_2_, ...), custom_call_target="tpu_custom_call" | custom-call | tf_op jit(solution)/shard_map/comm12/pallas_call | solution.py:295
  448.8 1.8 reduce_sum.319.refs_0_
  450.6 9.0 %comm13.1 = bf16[4,36,1536]{2,1,0:T(8,128)(2,1)} custom-call(bf16[36,1536]{1,0:T(8,128)(2,1)} %reduce_sum.319.refs_0_), custom_call_target="tpu_custom_call" | custom-call | tf_op jit(solution)/shard_map/comm13/pallas_call | solution.py:295
  459.6 1.1 select_convert_fusion
  464.8 1.2 copy.50
  (244 shorter events, 45.1 us)
Async XLA Ops:
  0.6 3.3 copy-start.46
  0.7 4.3 copy-start.63
  0.7 4.3 copy-start.64
  1.8 50.2 %copy-start.36 = (bf16[2,64,576]{2,1,0:T(8,128)(2,1)S(1)}, bf16[2,64,576]{2,1,0:T(8,128)(2,1)}, u32[]{:S(2)}) copy-start(bf16[2,64,576]{2,1,0:T(8,128)(2,1)} %param.12) | copy-start | bytes 442372
  75.2 26.6 %copy-start.9 = (bf16[2,576,384]{2,1,0:T(8,128)(2,1)S(1)}, bf16[2,576,384]{2,1,0:T(8,128)(2,1)}, u32[]{:S(2)}) copy-start(bf16[2,576,384]{2,1,0:T(8,128)(2,1)} %get-tuple-element.64) | copy-start | bytes 2654212
  86.0 17.3 %copy-start.19 = (bf16[2,576,384]{2,1,0:T(8,128)(2,1)S(1)}, bf16[2,576,384]{2,1,0:T(8,128)(2,1)}, u32[]{:S(2)}) copy-start(bf16[2,576,384]{2,1,0:T(8,128)(2,1)} %get-tuple-element.65) | copy-start | bytes 2654212
  101.8 4.3 copy-start.14
  103.2 2.2 copy-start.57
  105.5 0.7 copy-start.30
  117.9 120.5 %copy-start.10 = (bf16[64,576]{1,0:T(8,128)(2,1)}, bf16[64,576]{1,0:T(8,128)(2,1)S(1)}, u32[]{:S(2)}) copy-start(bf16[64,576]{1,0:T(8,128)(2,1)S(1)} %get-tuple-element.146.refs_0_) | copy-start | bytes 221188
  150.2 17.2 %copy-start.18 = (bf16[4,64,576]{2,1,0:T(8,128)(2,1)S(1)}, bf16[4,64,576]{2,1,0:T(8,128)(2,1)}, u32[]{:S(2)}) copy-start(bf16[4,64,576]{2,1,0:T(8,128)(2,1)} %get-tuple-element.68) | copy-start | bytes 884740
  151.9 30.6 %copy-start.12 = (f32[64,576]{1,0:T(8,128)}, f32[64,576]{1,0:T(8,128)S(1)}, u32[]{:S(2)}) copy-start(f32[64,576]{1,0:T(8,128)S(1)} %get-tuple-element.199) | copy-start | bytes 442372
  166.0 1.8 copy-start.1
  167.8 3.0 copy-start.20
  170.0 0.7 copy-start.26
  182.5 14.0 %copy-start.29 = (bf16[256,384]{1,0:T(8,128)(2,1)S(1)}, bf16[256,384]{1,0:T(8,128)(2,1)}, u32[]{:S(2)}) copy-start(bf16[256,384]{1,0:T(8,128)(2,1)} %copy-done.28) | copy-start | bytes 589828
  183.6 14.0 %copy-start.27 = (bf16[256,384]{1,0:T(8,128)(2,1)S(1)}, bf16[256,384]{1,0:T(8,128)(2,1)}, u32[]{:S(2)}) copy-start(bf16[256,384]{1,0:T(8,128)(2,1)} %copy-done.26) | copy-start | bytes 589828
  196.5 2.3 copy-start.32
  198.8 8.4 %copy-start.8 = (bf16[2048,384]{1,0:T(8,128)(2,1)S(1)}, bf16[2048,384]{1,0:T(8,128)(2,1)}, u32[]{:S(2)}) copy-start(bf16[2048,384]{1,0:T(8,128)(2,1)} %get-tuple-element.71) | copy-start | bytes 4718596
  209.4 25.6 %copy-start.39 = (f32[64,576]{1,0:T(8,128)S(1)}, f32[64,576]{1,0:T(8,128)}, u32[]{:S(2)}) copy-start(f32[64,576]{1,0:T(8,128)} %get-tuple-element.70) | copy-start | bytes 442372
  235.2 2.8 copy-start.60
  239.0 2.3 copy-start.6
  239.0 2.3 copy-start.56
  239.0 3.1 copy-start.5
  239.0 3.1 copy-start.55
  240.6 2.4 copy-start.3
  240.6 2.4 copy-start.41
  243.9 18.1 %copy-start.58 = (f32[256,384]{1,0:T(8,128)S(1)}, f32[256,384]{1,0:T(8,128)}, u32[]{:S(2)}) copy-start(f32[256,384]{1,0:T(8,128)} %copy-done.57) | copy-start | bytes 1179652
  262.0 2.5 copy-start.21
  263.7 0.7 copy-start.24
  263.7 0.7 copy-start.22
  273.0 12.1 %copy-start.16 = (bf16[64,576]{1,0:T(8,128)(2,1)S(1)}, bf16[64,576]{1,0:T(8,128)(2,1)}, u32[]{:S(2)}) copy-start(bf16[64,576]{1,0:T(8,128)(2,1)} %fusion.65.refs_0_.refs_3_) | copy-start | bytes 221188
  285.0 13.1 %copy-start.15 = (bf16[2,384,576]{2,1,0:T(8,128)(2,1)S(1)}, bf16[2,384,576]{2,1,0:T(8,128)(2,1)}, u32[]{:S(2)}) copy-start(bf16[2,384,576]{2,1,0:T(8,128)(2,1)} %get-tuple-element.66) | copy-start | bytes 2654212
  285.0 13.1 %copy-start.33 = (bf16[256,384]{1,0:T(8,128)(2,1)S(1)}, bf16[256,384]{1,0:T(8,128)(2,1)}, u32[]{:S(2)}) copy-start(bf16[256,384]{1,0:T(8,128)(2,1)} %get-tuple-element.155) | copy-start | bytes 589828
  287.4 12.0 %copy-start = (bf16[4,64,576]{2,1,0:T(8,128)(2,1)S(1)}, bf16[4,64,576]{2,1,0:T(8,128)(2,1)}, u32[]{:S(2)}) copy-start(bf16[4,64,576]{2,1,0:T(8,128)(2,1)} %comm2.2) | copy-start | bytes 884740
  287.4 12.0 %copy-start.25 = (bf16[256,384]{1,0:T(8,128)(2,1)S(1)}, bf16[256,384]{1,0:T(8,128)(2,1)}, u32[]{:S(2)}) copy-start(bf16[256,384]{1,0:T(8,128)(2,1)} %copy-done.24) | copy-start | bytes 589828
  287.4 13.1 %copy-start.23 = (bf16[256,384]{1,0:T(8,128)(2,1)S(1)}, bf16[256,384]{1,0:T(8,128)(2,1)}, u32[]{:S(2)}) copy-start(bf16[256,384]{1,0:T(8,128)(2,1)} %copy-done.22) | copy-start | bytes 589828
  298.1 3.5 copy-start.31
  298.5 5.3 %copy-start.50 = (bf16[4,144,384]{2,1,0:T(8,128)(2,1)S(1)}, bf16[4,144,384]{2,1,0:T(8,128)(2,1)}, u32[]{:S(2)}) copy-start(bf16[4,144,384]{2,1,0:T(8,128)(2,1)} %get-tuple-element.81) | copy-start | bytes 1327108
  299.4 5.1 %copy-start.49 = (bf16[4,144,384]{2,1,0:T(8,128)(2,1)S(1)}, bf16[4,144,384]{2,1,0:T(8,128)(2,1)}, u32[]{:S(2)}) copy-start(bf16[4,144,384]{2,1,0:T(8,128)(2,1)} %get-tuple-element.82) | copy-start | bytes 1327108
  300.5 4.7 %copy-start.42 = (bf16[4,96,576]{2,1,0:T(8,128)(2,1)S(1)}, bf16[4,96,576]{2,1,0:T(8,128)(2,1)}, u32[]{:S(2)}) copy-start(bf16[4,96,576]{2,1,0:T(8,128)(2,1)} %get-tuple-element.83) | copy-start | bytes 1327108
  306.0 17.7 %copy-start.13 = (f32[64,576]{1,0:T(8,128)S(1)}, f32[64,576]{1,0:T(8,128)}, u32[]{:S(2)}) copy-start(f32[64,576]{1,0:T(8,128)} %copy-done.12) | copy-start | bytes 442372
  306.0 18.4 %copy-start.7 = (bf16[2048,384]{1,0:T(8,128)(2,1)S(1)}, bf16[2048,384]{1,0:T(8,128)(2,1)}, u32[]{:S(2)}) copy-start(bf16[2048,384]{1,0:T(8,128)(2,1)} %get-tuple-element.80) | copy-start | bytes 4718596
  329.3 30.1 %copy-start.38 = (f32[64,576]{1,0:T(8,128)S(1)}, f32[64,576]{1,0:T(8,128)}, u32[]{:S(2)}) copy-start(f32[64,576]{1,0:T(8,128)} %get-tuple-element.85) | copy-start | bytes 442372
  359.0 0.9 copy-start.37
  359.6 3.0 copy-start.59
  365.2 4.4 copy-start.4
  365.2 6.3 %copy-start.2 = (bf16[384,576]{1,0:T(8,128)(2,1)S(1)}, bf16[384,576]{1,0:T(8,128)(2,1)}, u32[]{:S(2)}) copy-start(bf16[384,576]{1,0:T(8,128)(2,1)} %convolution_convert_fusion.4.refs_4_) | copy-start | bytes 1327108
  373.4 20.0 %copy-start.11 = (bf16[64,576]{1,0:T(8,128)(2,1)S(1)}, bf16[64,576]{1,0:T(8,128)(2,1)}, u32[]{:S(2)}) copy-start(bf16[64,576]{1,0:T(8,128)(2,1)} %copy-done.10) | copy-start | bytes 221188
  373.4 20.0 %copy-start.35 = (bf16[64,576]{1,0:T(8,128)(2,1)S(1)}, bf16[64,576]{1,0:T(8,128)(2,1)}, u32[]{:S(2)}) copy-start(bf16[64,576]{1,0:T(8,128)(2,1)} %add_convert_fusion.8.refs_1_) | copy-start | bytes 221188
  373.4 21.7 %copy-start.17 = (bf16[64,576]{1,0:T(8,128)(2,1)S(1)}, bf16[64,576]{1,0:T(8,128)(2,1)}, u32[]{:S(2)}) copy-start(bf16[64,576]{1,0:T(8,128)(2,1)} %fusion.65.refs_0_.refs_3_) | copy-start | bytes 221188
  373.4 21.7 %copy-start.34 = (bf16[64,576]{1,0:T(8,128)(2,1)S(1)}, bf16[64,576]{1,0:T(8,128)(2,1)}, u32[]{:S(2)}) copy-start(bf16[64,576]{1,0:T(8,128)(2,1)} %fusion.54.refs_2_) | copy-start | bytes 221188
  402.6 1.5 copy-start.61
  402.6 1.5 copy-start.62
  427.1 4.5 copy-start.52
  427.1 5.2 %copy-start.51 = (bf16[4,144,384]{2,1,0:T(8,128)(2,1)S(1)}, bf16[4,144,384]{2,1,0:T(8,128)(2,1)}, u32[]{:S(2)}) copy-start(bf16[4,144,384]{2,1,0:T(8,128)(2,1)} %get-tuple-element.101) | copy-start | bytes 1327108
  428.8 4.3 copy-start.43
  431.6 28.0 %copy-start.40 = (bf16[4,36,1536]{2,1,0:T(8,128)(2,1)S(1)}, bf16[4,36,1536]{2,1,0:T(8,128)(2,1)}, u32[]{:S(2)}) copy-start(bf16[4,36,1536]{2,1,0:T(8,128)(2,1)} %get-tuple-element.104) | copy-start | bytes 1327108
  460.7 1.9 copy-start.48
  460.8 1.9 copy-start.54
  461.8 1.8 copy-start.47
  461.8 1.8 copy-start.53
  462.7 2.0 copy-start.44
  462.7 2.0 copy-start.45
  (1 other events, 0.7 us)

commit v3 on v2

--- a/solution.py
+++ b/solution.py
@@ -509,7 +509,7 @@
         r2 = lax.rsqrt(jnp.mean(h2 * h2, -1, keepdims=True) + EPS)
         n2 = h2 * r2
         z = (n2 * gm).astype(BF)
-        (zr,) = communicate(sizes, ("chain", (), z))
+        (zr,) = communicate(sizes, ("ag", ("wt",), z))
         zr = zr.reshape(n_wt * rows, width)
         g = nn(zr, gates[layer])
         up = nn(zr, ups[layer])
@@ -553,7 +553,7 @@
         if layer == 0:
             er, attn1_theirs, gain1_theirs, *mlp1 = communicate(
                 sizes,
-                ("chain", (), e),
+                ("ag", ("wt",), e),
                 ("to", (), attn1, 1),
                 ("to", (), gain1, 1),
                 *many("a2a", ctx, mlp_chunks(mlp1), 1),

time: 468 us -> 469 us (level)
  no operation moved by 1% of the time
where the time goes in v3:
time: 469 us; the launch traced here: 467 us
  Pallas kernels  341 us (73%)
  other arithmetic  63.4 us (14%)
  matrix products  36.1 us (8%)
  local copies, waits for them, and re-layouts  25.4 us (5%)
    pallas_call x17, Pallas kernels, communicate(): pl.pallas_call(functools.partial(comm_kernel, tuple(plan), sizes, len(arr...  300 us
    pallas_call x2, Pallas kernels, attend_back(): pl.pallas_call(functools.partial(attend_back_kernel, 512 if keys % 512 ==...  21.3 us
    reduce_sum x16, other arithmetic, total(): return jnp.sum(x.astype(F32), 0)  20.1 us
    convert_element_type x10, other arithmetic, summed(): return (own.astype(F32) + other.astype(F32)).astype(BF)  19.8 us
    pallas_call x2, Pallas kernels, attend(): pl.pallas_call(functools.partial(attend_kernel, 512 if keys % 512 == 0 el...  18.8 us
    dot_general x10, matrix products, nn(): return jnp.dot(a, b, preferred_element_type=F32)  14.8 us
    dot_general x10, matrix products, nt(): lax.dot_general(a, b, (((1,), (1,)), ((), ())), preferred_element_type=F32)  11.7 us
    dot_general x10, matrix products, tn(): lax.dot_general(a, b, (((0,), (0,)), ((), ())), preferred_element_type=F32)  9.61 us

profile of v3, /device:TPU:0, one launch (start us, length us, event | category | flops | bytes accessed | tf_op | source)
XLA Modules:
  0.0 467.1 jit_solution(13713266736420318864)
XLA Ops:
  1.8 2.1 concatenate.106.refs_0_
  5.5 1.6 bitcast_convert_fusion.3.refs_5_
  7.1 44.1 %comm0.1 = (bf16[2,4,144,1536]{3,2,1,0:T(8,128)(2,1)}, bf16[2,576,384]{2,1,0:T(8,128)(2,1)}, bf16[2,576,384]{2,1,0:T(8,128)(2,1)}, bf16[2,384,576]{2,1,0:T(8,128...) custom-call(bf16[144,1536]{1,0:T(8,128)(2,1)} %concatenate.106.refs_0_, bf16[576,384]{1,0:T(8,128)(2,1)} %bitcast.244, ...), custom_call_target="tpu_custom_call" | custom-call | tf_op jit(solution)/shard_map/comm0/pallas_call | solution.py:295
  52.2 1.7 fusion.5
  56.0 19.2 %comm1.2 = bf16[2,4,4,64,384]{4,3,2,1,0:T(8,128)(2,1)} custom-call(bf16[64,384]{1,0:T(8,128)(2,1)} %pad_maximum_fusion.4.refs_0_), custom_call_target="tpu_custom_call" | custom-call | tf_op jit(solution)/shard_map/comm1/pallas_call | solution.py:295
  76.5 9.4 %attend.2 = (bf16[64,576]{1,0:T(8,128)(2,1)}, f32[3,192]{1,0:T(4,128)}) custom-call(bf16[64,576]{1,0:T(8,128)(2,1)} %fusion.71.q_ref, bf16[2048,384]{1,0:T(8,128)(2,1)} %bitcast.196, s32[1,192]{1,0:T(1,128)} %broadcast_in_dim_tile.6.pos_ref, s32[1,192]{1,0:T(1,128)} %broadcast_in_dim_tile.7.doc_ref), custom_call_target="tpu_custom_call" | custom-call | tf_op jit(solution)/shard_map/attend/pallas_call | solution.py:371
  86.0 1.8 multiply_reduce_fusion.5
  88.5 11.5 %comm2.2 = bf16[4,64,576]{2,1,0:T(8,128)(2,1)} custom-call(bf16[64,576]{1,0:T(8,128)(2,1)} %multiply_convert_fusion.7.refs_0_), custom_call_target="tpu_custom_call" | custom-call | tf_op jit(solution)/shard_map/comm2/pallas_call | solution.py:295
  100.1 1.4 fusion.26
  101.5 2.2 multiply_convert_fusion.5
  105.7 11.3 %comm3.2 = bf16[4,64,576]{2,1,0:T(8,128)(2,1)} custom-call(bf16[4,64,576]{2,1,0:T(8,128)(2,1)} %bitcast.236), custom_call_target="tpu_custom_call" | custom-call | tf_op jit(solution)/shard_map/comm3/pallas_call | solution.py:295
  118.2 1.7 fusion.7
  121.8 19.8 %comm1.3 = bf16[2,4,4,64,384]{4,3,2,1,0:T(8,128)(2,1)} custom-call(bf16[64,384]{1,0:T(8,128)(2,1)} %pad_maximum_fusion.5.refs_0_), custom_call_target="tpu_custom_call" | custom-call | tf_op jit(solution)/shard_map/comm1/pallas_call | solution.py:295
  141.6 9.4 %attend.3 = (bf16[64,576]{1,0:T(8,128)(2,1)}, f32[3,192]{1,0:T(4,128)}) custom-call(bf16[64,576]{1,0:T(8,128)(2,1)} %fusion.69.q_ref, bf16[2048,384]{1,0:T(8,128)(2,1)} %bitcast.198, s32[1,192]{1,0:T(1,128)} %broadcast_in_dim_tile.6.pos_ref, s32[1,192]{1,0:T(1,128)} %broadcast_in_dim_tile.7.doc_ref), custom_call_target="tpu_custom_call" | custom-call | tf_op jit(solution)/shard_map/attend/pallas_call | solution.py:371
  151.0 1.7 multiply_reduce_fusion.4
  153.5 11.6 %comm2.3 = bf16[4,64,576]{2,1,0:T(8,128)(2,1)} custom-call(bf16[64,576]{1,0:T(8,128)(2,1)} %multiply_convert_fusion.6.refs_0_), custom_call_target="tpu_custom_call" | custom-call | tf_op jit(solution)/shard_map/comm2/pallas_call | solution.py:295
  165.1 1.4 fusion.16
  166.8 2.2 multiply_convert_fusion.2
  171.1 11.3 %comm3.3 = bf16[4,64,576]{2,1,0:T(8,128)(2,1)} custom-call(bf16[4,64,576]{2,1,0:T(8,128)(2,1)} %bitcast.237), custom_call_target="tpu_custom_call" | custom-call | tf_op jit(solution)/shard_map/comm3/pallas_call | solution.py:295
  184.7 2.2 convolution_convert_fusion.13.do_ref
  187.0 10.6 %attend_back.2 = (f32[64,576]{1,0:T(8,128)}, bf16[2048,384]{1,0:T(8,128)(2,1)}) custom-call(bf16[64,576]{1,0:T(8,128)(2,1)} %fusion.69.q_ref, bf16[64,576]{1,0:T(8,128)(2,1)} %convolution_convert_fusion.13.do_ref, bf16[64,576]{1,0:T(8,128)(2,1)} %get-tuple-element.67.o_ref, bf16[2048,384]{1,0:T(8,128)(2,1)} %bitcast.199, ...), custom_call_target="tpu_custom_call" | custom-call | tf_op jit(solution)/shard_map/attend_back/pallas_call | solution.py:424
  198.7 1.1 convolution_convert_fusion.8.refs_2_
  199.8 1.1 convolution_convert_fusion.5.refs_3_
  201.0 7.2 %comm4.1 = (bf16[16,64,384]{2,1,0:T(8,128)(2,1)}, bf16[576,384]{1,0:T(8,128)(2,1)}, bf16[576,384]{1,0:T(8,128)(2,1)}, bf16[384,576]{1,0:T(8,128)(2,1)}) custom-call(bf16[2,16,64,384]{3,2,1,0:T(8,128)(2,1)} %bitcast.220, bf16[576,384]{1,0:T(8,128)(2,1)} %convolution_convert_fusion.9.refs_1_, bf16[576,384]{1,0:T(8,128)(2,1)} %convolution_convert_fusion.8.refs_2_, ...), custom_call_target="tpu_custom_call" | custom-call | tf_op jit(solution)/shard_map/comm4/pallas_call | solution.py:295
  208.2 2.2 fusion.1.refs_0_
  210.5 24.7 %comm5.1 = bf16[16,64,384]{2,1,0:T(8,128)(2,1)} custom-call(bf16[16,64,384]{2,1,0:T(8,128)(2,1)} %fusion.1.refs_0_), custom_call_target="tpu_custom_call" | custom-call | tf_op jit(solution)/shard_map/comm5/pallas_call | solution.py:295
  235.1 1.3 convert_reduce_fusion.1
  237.1 1.9 fusion.66
  240.8 1.6 pad_maximum_fusion.refs_1_
  245.6 14.6 %comm6.1 = (bf16[4,64,576]{2,1,0:T(8,128)(2,1)}, bf16[576,1536]{1,0:T(8,128)(2,1)}, f32[2,576]{1,0:T(2,128)}, bf16[4,144,384]{2,1,0:T(8,128)(2,1)}, bf16[4,144,3...) custom-call(bf16[64,576]{1,0:T(8,128)(2,1)} %fusion.65.refs_0_.refs_3_, bf16[576,1536]{1,0:T(8,128)(2,1)} %pad_maximum_fusion.refs_1_, ...), custom_call_target="tpu_custom_call" | custom-call | tf_op jit(solution)/shard_map/comm6/pallas_call | solution.py:295
  260.3 1.7 multiply_convert_fusion
  264.0 3.4 add_convert_fusion.1
  267.4 2.4 reshape.410
  269.8 1.5 copy.56
  271.3 14.1 %comm7.1 = (bf16[4,64,576]{2,1,0:T(8,128)(2,1)}, bf16[4,4,36,1536]{3,2,1,0:T(8,128)(2,1)}) custom-call(bf16[4,64,576]{2,1,0:T(8,128)(2,1)} %bitcast.235, bf16[4,4,36,1536]{3,2,1,0:T(8,128)(2,1)} %bitcast.201), custom_call_target="tpu_custom_call" | custom-call | tf_op jit(solution)/shard_map/comm7/pallas_call | solution.py:295
  286.8 2.3 convolution_convert_fusion.12.do_ref
  289.1 10.7 %attend_back.3 = (f32[64,576]{1,0:T(8,128)}, bf16[2048,384]{1,0:T(8,128)(2,1)}) custom-call(bf16[64,576]{1,0:T(8,128)(2,1)} %fusion.71.q_ref, bf16[64,576]{1,0:T(8,128)(2,1)} %convolution_convert_fusion.12.do_ref, bf16[64,576]{1,0:T(8,128)(2,1)} %get-tuple-element.63.o_ref, bf16[2048,384]{1,0:T(8,128)(2,1)} %bitcast.197, ...), custom_call_target="tpu_custom_call" | custom-call | tf_op jit(solution)/shard_map/attend_back/pallas_call | solution.py:424
  301.0 1.1 convolution_convert_fusion.7.refs_2_
  302.2 1.1 convolution_convert_fusion.6.refs_3_
  303.3 2.1 convolution_convert_fusion.4.refs_4_
  307.6 17.2 %comm8.1 = (bf16[16,64,384]{2,1,0:T(8,128)(2,1)}, bf16[4,64,576]{2,1,0:T(8,128)(2,1)}, bf16[576,384]{1,0:T(8,128)(2,1)}, bf16[576,384]{1,0:T(8,128)(2,1)}, bf16[...) custom-call(bf16[2,16,64,384]{3,2,1,0:T(8,128)(2,1)} %bitcast.218, ...), custom_call_target="tpu_custom_call" | custom-call | tf_op jit(solution)/shard_map/comm8/pallas_call | solution.py:295
  326.5 2.2 fusion.refs_0_
  328.7 2.8 reduce_sum.308.refs_1_
  331.5 27.1 %comm9.1 = (bf16[16,64,384]{2,1,0:T(8,128)(2,1)}, bf16[4,36,1536]{2,1,0:T(8,128)(2,1)}) custom-call(bf16[16,64,384]{2,1,0:T(8,128)(2,1)} %fusion.refs_0_, bf16[4,36,1536]{2,1,0:T(8,128)(2,1)} %reduce_sum.308.refs_1_), custom_call_target="tpu_custom_call" | custom-call | tf_op jit(solution)/shard_map/comm9/pallas_call | solution.py:295
  358.6 1.3 convert_reduce_fusion
  360.7 1.9 fusion.56
  364.3 1.6 pad_maximum_fusion.1.refs_4_
  366.6 1.8 reduce_sum.313.refs_6_
  368.4 2.0 add_convert_fusion.5
  370.4 1.9 add_convert_fusion.4
  372.3 1.9 add_convert_fusion.2
  374.3 20.8 %comm10.1 = (bf16[64,576]{1,0:T(8,128)(2,1)}, bf16[64,576]{1,0:T(8,128)(2,1)}, bf16[576,1536]{1,0:T(8,128)(2,1)}, f32[2,576]{1,0:T(2,128)}, bf16[4,36,1536]{2,1,...) custom-call(bf16[64,576]{1,0:T(8,128)(2,1)} %copy-done.10, ...), custom_call_target="tpu_custom_call" | custom-call | tf_op jit(solution)/shard_map/comm10/pallas_call | solution.py:295
  395.1 1.7 maximum_select_fusion.2
  396.8 1.7 maximum_select_fusion.3
  398.5 3.4 add_convert_fusion
  401.9 2.4 reshape.416
  404.3 1.5 copy.55
  406.4 21.8 %comm11.1 = (bf16[4,4,36,1536]{3,2,1,0:T(8,128)(2,1)}, f32[16,2,576]{2,1,0:T(2,128)}) custom-call(bf16[4,4,36,1536]{3,2,1,0:T(8,128)(2,1)} %bitcast.200, f32[2,576]{1,0:T(2,128)} %add_select_fusion.1.refs_1_), custom_call_target="tpu_custom_call" | custom-call | tf_op jit(solution)/shard_map/comm11/pallas_call | solution.py:295
  429.9 2.8 reduce_sum.315.refs_0_
  434.9 15.0 %comm12.1 = (bf16[4,36,1536]{2,1,0:T(8,128)(2,1)}, bf16[4,144,384]{2,1,0:T(8,128)(2,1)}, bf16[4,144,384]{2,1,0:T(8,128)(2,1)}, bf16[4,96,576]{2,1,0:T(8,128)(2,1)}) custom-call(bf16[4,36,1536]{2,1,0:T(8,128)(2,1)} %reduce_sum.315.refs_0_, bf16[144,384]{1,0:T(8,128)(2,1)} %reduce_sum.316.refs_1_, bf16[144,384]{1,0:T(8,128)(2,1)} %reduce_sum.317.refs_2_, ...), custom_call_target="tpu_custom_call" | custom-call | tf_op jit(solution)/shard_map/comm12/pallas_call | solution.py:295
  449.9 1.8 reduce_sum.319.refs_0_
  451.7 9.0 %comm13.1 = bf16[4,36,1536]{2,1,0:T(8,128)(2,1)} custom-call(bf16[36,1536]{1,0:T(8,128)(2,1)} %reduce_sum.319.refs_0_), custom_call_target="tpu_custom_call" | custom-call | tf_op jit(solution)/shard_map/comm13/pallas_call | solution.py:295
  460.7 1.1 select_convert_fusion
  465.9 1.2 copy.50
  (244 shorter events, 45.1 us)
Async XLA Ops:
  0.6 3.3 copy-start.46
  0.7 4.3 copy-start.63
  0.7 4.3 copy-start.64
  1.8 50.2 %copy-start.36 = (bf16[2,64,576]{2,1,0:T(8,128)(2,1)S(1)}, bf16[2,64,576]{2,1,0:T(8,128)(2,1)}, u32[]{:S(2)}) copy-start(bf16[2,64,576]{2,1,0:T(8,128)(2,1)} %param.12) | copy-start | bytes 442372
  75.2 24.8 %copy-start.9 = (bf16[2,576,384]{2,1,0:T(8,128)(2,1)S(1)}, bf16[2,576,384]{2,1,0:T(8,128)(2,1)}, u32[]{:S(2)}) copy-start(bf16[2,576,384]{2,1,0:T(8,128)(2,1)} %get-tuple-element.64) | copy-start | bytes 2654212
  86.0 15.5 %copy-start.19 = (bf16[2,576,384]{2,1,0:T(8,128)(2,1)S(1)}, bf16[2,576,384]{2,1,0:T(8,128)(2,1)}, u32[]{:S(2)}) copy-start(bf16[2,576,384]{2,1,0:T(8,128)(2,1)} %get-tuple-element.65) | copy-start | bytes 2654212
  100.0 4.3 copy-start.14
  101.4 2.2 copy-start.57
  103.7 0.7 copy-start.30
  118.1 122.0 %copy-start.10 = (bf16[64,576]{1,0:T(8,128)(2,1)}, bf16[64,576]{1,0:T(8,128)(2,1)S(1)}, u32[]{:S(2)}) copy-start(bf16[64,576]{1,0:T(8,128)(2,1)S(1)} %get-tuple-element.146.refs_0_) | copy-start | bytes 221188
  151.0 15.5 %copy-start.18 = (bf16[4,64,576]{2,1,0:T(8,128)(2,1)S(1)}, bf16[4,64,576]{2,1,0:T(8,128)(2,1)}, u32[]{:S(2)}) copy-start(bf16[4,64,576]{2,1,0:T(8,128)(2,1)} %get-tuple-element.68) | copy-start | bytes 884740
  152.7 30.9 %copy-start.12 = (f32[64,576]{1,0:T(8,128)}, f32[64,576]{1,0:T(8,128)S(1)}, u32[]{:S(2)}) copy-start(f32[64,576]{1,0:T(8,128)S(1)} %get-tuple-element.199) | copy-start | bytes 442372
  165.1 1.8 copy-start.1
  166.8 3.0 copy-start.20
  169.1 0.7 copy-start.26
  183.6 14.0 %copy-start.29 = (bf16[256,384]{1,0:T(8,128)(2,1)S(1)}, bf16[256,384]{1,0:T(8,128)(2,1)}, u32[]{:S(2)}) copy-start(bf16[256,384]{1,0:T(8,128)(2,1)} %copy-done.28) | copy-start | bytes 589828
  184.7 14.0 %copy-start.27 = (bf16[256,384]{1,0:T(8,128)(2,1)S(1)}, bf16[256,384]{1,0:T(8,128)(2,1)}, u32[]{:S(2)}) copy-start(bf16[256,384]{1,0:T(8,128)(2,1)} %copy-done.26) | copy-start | bytes 589828
  197.6 2.3 copy-start.32
  199.8 8.4 %copy-start.8 = (bf16[2048,384]{1,0:T(8,128)(2,1)S(1)}, bf16[2048,384]{1,0:T(8,128)(2,1)}, u32[]{:S(2)}) copy-start(bf16[2048,384]{1,0:T(8,128)(2,1)} %get-tuple-element.71) | copy-start | bytes 4718596
  210.5 26.3 %copy-start.39 = (f32[64,576]{1,0:T(8,128)S(1)}, f32[64,576]{1,0:T(8,128)}, u32[]{:S(2)}) copy-start(f32[64,576]{1,0:T(8,128)} %get-tuple-element.70) | copy-start | bytes 442372
  237.0 2.8 copy-start.60
  240.7 2.3 copy-start.6
  240.7 2.3 copy-start.56
  240.7 3.1 copy-start.5
  240.8 3.1 copy-start.55
  242.4 2.4 copy-start.3
  242.4 2.4 copy-start.41
  245.6 14.6 %copy-start.58 = (f32[256,384]{1,0:T(8,128)S(1)}, f32[256,384]{1,0:T(8,128)}, u32[]{:S(2)}) copy-start(f32[256,384]{1,0:T(8,128)} %copy-done.57) | copy-start | bytes 1179652
  260.3 2.5 copy-start.21
  262.0 0.7 copy-start.24
  262.1 0.7 copy-start.22
  271.3 15.4 %copy-start.16 = (bf16[64,576]{1,0:T(8,128)(2,1)S(1)}, bf16[64,576]{1,0:T(8,128)(2,1)}, u32[]{:S(2)}) copy-start(bf16[64,576]{1,0:T(8,128)(2,1)} %fusion.65.refs_0_.refs_3_) | copy-start | bytes 221188
  286.6 13.1 %copy-start.15 = (bf16[2,384,576]{2,1,0:T(8,128)(2,1)S(1)}, bf16[2,384,576]{2,1,0:T(8,128)(2,1)}, u32[]{:S(2)}) copy-start(bf16[2,384,576]{2,1,0:T(8,128)(2,1)} %get-tuple-element.66) | copy-start | bytes 2654212
  286.6 13.1 %copy-start.33 = (bf16[256,384]{1,0:T(8,128)(2,1)S(1)}, bf16[256,384]{1,0:T(8,128)(2,1)}, u32[]{:S(2)}) copy-start(bf16[256,384]{1,0:T(8,128)(2,1)} %get-tuple-element.155) | copy-start | bytes 589828
  289.0 12.0 %copy-start = (bf16[4,64,576]{2,1,0:T(8,128)(2,1)S(1)}, bf16[4,64,576]{2,1,0:T(8,128)(2,1)}, u32[]{:S(2)}) copy-start(bf16[4,64,576]{2,1,0:T(8,128)(2,1)} %comm2.2) | copy-start | bytes 884740
  289.1 12.0 %copy-start.25 = (bf16[256,384]{1,0:T(8,128)(2,1)S(1)}, bf16[256,384]{1,0:T(8,128)(2,1)}, u32[]{:S(2)}) copy-start(bf16[256,384]{1,0:T(8,128)(2,1)} %copy-done.24) | copy-start | bytes 589828
  289.1 13.1 %copy-start.23 = (bf16[256,384]{1,0:T(8,128)(2,1)S(1)}, bf16[256,384]{1,0:T(8,128)(2,1)}, u32[]{:S(2)}) copy-start(bf16[256,384]{1,0:T(8,128)(2,1)} %copy-done.22) | copy-start | bytes 589828
  299.7 3.5 copy-start.31
  300.1 5.3 %copy-start.50 = (bf16[4,144,384]{2,1,0:T(8,128)(2,1)S(1)}, bf16[4,144,384]{2,1,0:T(8,128)(2,1)}, u32[]{:S(2)}) copy-start(bf16[4,144,384]{2,1,0:T(8,128)(2,1)} %get-tuple-element.81) | copy-start | bytes 1327108
  301.0 5.1 %copy-start.49 = (bf16[4,144,384]{2,1,0:T(8,128)(2,1)S(1)}, bf16[4,144,384]{2,1,0:T(8,128)(2,1)}, u32[]{:S(2)}) copy-start(bf16[4,144,384]{2,1,0:T(8,128)(2,1)} %get-tuple-element.82) | copy-start | bytes 1327108
  302.2 4.7 %copy-start.42 = (bf16[4,96,576]{2,1,0:T(8,128)(2,1)S(1)}, bf16[4,96,576]{2,1,0:T(8,128)(2,1)}, u32[]{:S(2)}) copy-start(bf16[4,96,576]{2,1,0:T(8,128)(2,1)} %get-tuple-element.83) | copy-start | bytes 1327108
  307.6 18.3 %copy-start.13 = (f32[64,576]{1,0:T(8,128)S(1)}, f32[64,576]{1,0:T(8,128)}, u32[]{:S(2)}) copy-start(f32[64,576]{1,0:T(8,128)} %copy-done.12) | copy-start | bytes 442372
  307.6 18.9 %copy-start.7 = (bf16[2048,384]{1,0:T(8,128)(2,1)S(1)}, bf16[2048,384]{1,0:T(8,128)(2,1)}, u32[]{:S(2)}) copy-start(bf16[2048,384]{1,0:T(8,128)(2,1)} %get-tuple-element.80) | copy-start | bytes 4718596
  331.5 28.7 %copy-start.38 = (f32[64,576]{1,0:T(8,128)S(1)}, f32[64,576]{1,0:T(8,128)}, u32[]{:S(2)}) copy-start(f32[64,576]{1,0:T(8,128)} %get-tuple-element.85) | copy-start | bytes 442372
  359.8 0.9 copy-start.37
  360.4 3.0 copy-start.59
  366.0 4.4 copy-start.4
  366.0 6.3 %copy-start.2 = (bf16[384,576]{1,0:T(8,128)(2,1)S(1)}, bf16[384,576]{1,0:T(8,128)(2,1)}, u32[]{:S(2)}) copy-start(bf16[384,576]{1,0:T(8,128)(2,1)} %convolution_convert_fusion.4.refs_4_) | copy-start | bytes 1327108
  374.2 20.9 %copy-start.11 = (bf16[64,576]{1,0:T(8,128)(2,1)S(1)}, bf16[64,576]{1,0:T(8,128)(2,1)}, u32[]{:S(2)}) copy-start(bf16[64,576]{1,0:T(8,128)(2,1)} %copy-done.10) | copy-start | bytes 221188
  374.2 20.9 %copy-start.35 = (bf16[64,576]{1,0:T(8,128)(2,1)S(1)}, bf16[64,576]{1,0:T(8,128)(2,1)}, u32[]{:S(2)}) copy-start(bf16[64,576]{1,0:T(8,128)(2,1)} %add_convert_fusion.8.refs_1_) | copy-start | bytes 221188
  374.2 22.6 %copy-start.17 = (bf16[64,576]{1,0:T(8,128)(2,1)S(1)}, bf16[64,576]{1,0:T(8,128)(2,1)}, u32[]{:S(2)}) copy-start(bf16[64,576]{1,0:T(8,128)(2,1)} %fusion.65.refs_0_.refs_3_) | copy-start | bytes 221188
  374.2 22.6 %copy-start.34 = (bf16[64,576]{1,0:T(8,128)(2,1)S(1)}, bf16[64,576]{1,0:T(8,128)(2,1)}, u32[]{:S(2)}) copy-start(bf16[64,576]{1,0:T(8,128)(2,1)} %fusion.54.refs_2_) | copy-start | bytes 221188
  404.3 1.5 copy-start.61
  404.3 1.5 copy-start.62
  428.2 4.5 copy-start.52
  428.2 5.2 %copy-start.51 = (bf16[4,144,384]{2,1,0:T(8,128)(2,1)S(1)}, bf16[4,144,384]{2,1,0:T(8,128)(2,1)}, u32[]{:S(2)}) copy-start(bf16[4,144,384]{2,1,0:T(8,128)(2,1)} %get-tuple-element.101) | copy-start | bytes 1327108
  429.9 4.3 copy-start.43
  432.7 28.0 %copy-start.40 = (bf16[4,36,1536]{2,1,0:T(8,128)(2,1)S(1)}, bf16[4,36,1536]{2,1,0:T(8,128)(2,1)}, u32[]{:S(2)}) copy-start(bf16[4,36,1536]{2,1,0:T(8,128)(2,1)} %get-tuple-element.104) | copy-start | bytes 1327108
  461.8 1.9 copy-start.48
  461.8 1.9 copy-start.54
  462.9 1.8 copy-start.47
  462.9 1.8 copy-start.53
  463.7 2.0 copy-start.44
  463.7 2.0 copy-start.45
  (1 other events, 0.7 us)
